TPU v7x, 32 devices: a whole 2x2x4 slice. The times are simulated.
32 devices in a mesh: series: 4 (over y, x), tm: 8 (over z, core).
Axes of the slice: x: 2, y: 2, z: 4, core: 2. Of those that a mesh axis runs over, the one named last changes fastest.
Arguments:
- observed: bfloat16 [8192, 8192], P('series', 'tm'), may hold values from -6 to 6
- mask: bfloat16 [8192, 8192], P('series', 'tm'), may hold values from 0 to 1, as said below
- loadings: float32 [8192, 128], P('series'), may hold values from -0.5 to 0.5
- factors: float32 [8192, 128], P('tm'), may hold values from -6 to 6
- lag_weights: float32 [2, 128], replicated, may hold values from 0.2 to 0.7
Outputs:
- new_loadings: float32 [8192, 128], P('series')
- new_factors: float32 [8192, 128], P('tm')
Inputs may be any that keep to these rules, and one draw needn't show every extreme that they name: `mask`: each entry is 0 or 1.
All inputs are finite; a program needn't handle non-finite values.
Results may differ from a plain program's by a relative error of at most 0.0041.
Values sent between devices are 32-bit elements; how exact they have to be, the bound alone decides.
No kernel may reach another device: no remote copies, remote signals or barrier semaphores. Data moves between devices by JAX's collectives and lax.ppermute only.
A program may use at most 128 MiB of HBM per device.

v0:
```python
import jax
import jax.numpy as jnp
from jax import lax
from jax.sharding import PartitionSpec as P

LAG = 1440
OUTER = 2
TIME_STEPS = 2


smooth = 4.0
shrink = 0.1
margin = 32.0


def shifted(value, axis, steps):
    count = lax.axis_size(axis)
    initial, last = (max(0, -steps), min(count, count - steps))
    return lax.ppermute(value, axis, [(source, source + steps) for source in range(initial, last)])


def tile_residual(observed, mask, fb, xb):
    prod = lax.dot_general(fb, xb, (((1,), (1,)), ((), ())), preferred_element_type=jnp.float32)
    return (mask.astype(jnp.float32) * (prod - observed.astype(jnp.float32))).astype(jnp.bfloat16)


def smoothing(times, lag_weights):
    minutes = times.shape[0]
    whole = LAG // minutes
    rest = LAG % minutes
    before_one = jnp.concatenate(
        [shifted(times[minutes - 1 :], "tm", 1), times[: minutes - 1]], axis=0
    )
    before_far = jnp.concatenate(
        [
            shifted(times[minutes - rest :], "tm", whole + 1),
            shifted(times[: minutes - rest], "tm", whole),
        ],
        axis=0,
    )
    resid = times - lag_weights[0] * before_one - lag_weights[1] * before_far
    after_one = jnp.concatenate([resid[1:], shifted(resid[:1], "tm", -1)], axis=0)
    after_far = jnp.concatenate(
        [shifted(resid[rest:], "tm", -whole), shifted(resid[:rest], "tm", -(whole + 1))], axis=0
    )
    return smooth * (resid - lag_weights[0] * after_one - lag_weights[1] * after_far)


def body(observed, mask, loadings, factors, lag_weights):
    total_series = loadings.shape[0] * lax.axis_size("series")
    total_minutes = factors.shape[0] * lax.axis_size("tm")
    rank_width = loadings.shape[1]
    step_time = 1.0 / (total_series / rank_width + margin)
    step_load = 1.0 / total_minutes
    loads = loadings
    times = factors
    for outer in range(OUTER):
        fb = loads.astype(jnp.bfloat16)
        for inner in range(TIME_STEPS):
            xb = times.astype(jnp.bfloat16)
            rb = tile_residual(observed, mask, fb, xb)
            partial_grad = lax.dot_general(
                rb, fb, (((0,), (0,)), ((), ())), preferred_element_type=jnp.float32
            )
            smooth_grad = smoothing(times, lag_weights)
            share = lax.psum_scatter(partial_grad, "series", scatter_dimension=0, tiled=True)
            rows = share.shape[0]
            start = lax.axis_index("series") * rows
            own = lax.dynamic_slice_in_dim(times, start, rows, 0)
            own_smooth = lax.dynamic_slice_in_dim(smooth_grad, start, rows, 0)
            updated = own - step_time * (share + own_smooth)
            times = lax.all_gather(updated, "series", axis=0, tiled=True)
        xb = times.astype(jnp.bfloat16)
        rb = tile_residual(observed, mask, fb, xb)
        partial_load = jnp.dot(rb, xb, preferred_element_type=jnp.float32)
        grad_f = lax.psum(partial_load, "tm")
        loads = loads - step_load * (grad_f + shrink * loads)
    return (loads, times)


def solution(mesh):
    in_specs = (P("series", "tm"), P("series", "tm"), P("series", None), P("tm", None), P())
    out_specs = (P("series", None), P("tm", None))
    return jax.shard_map(body, mesh=mesh, in_specs=in_specs, out_specs=out_specs, check_vma=False)
```

profile of v0, /device:TPU:0, one launch (start us, length us, event | category | flops | bytes accessed | tf_op | source)
XLA Modules:
  0.0 333.9 jit_solution(2569922140256793986)
XLA Ops:
  7.2 9.1 %fusion.11 = f32[1024,128]{1,0:T(8,128)} fusion(bf16[2048,1024]{1,0:T(8,128)(2,1)} %param.6, bf16[2048,1024]{1,0:T(8,128)(2,1)} %param.5, f32[1024,128]{1,0:T(8,128)} %param.8, f32[2048,128]{1,0:T(8,128)} %param.7), kind=kOutput, calls=%fused_computation.23 | convolution fusion | flops 1084882944 | bytes 10485760 | tf_op jit(solution)/shard_map/dot_general | solution.py:62
  16.4 2.5 collective-permute-start.2
  19.0 4.6 %collective-permute-start = (f32[1,128]{1,0:T(1,128)S(1)}, f32[1,128]{1,0:T(1,128)S(1)}, u32[]{:S(2)}, u32[]{:S(2)}) collective-permute-start(f32[1,128]{1,0:T(1,128)S(1)} %slice.117), channel_id=1, source_target_pairs={{0,1},{1,2},{2,3},{3,4},{4,5},{5,6},{6,7},{8,9},{9,10},{10,11},{11... | collective-permute-start | bytes 1544 | tf_op jit(solution)/shard_map/ppermute | solution.py:19
  23.6 3.5 %collective-permute-start.1 = (f32[416,128]{1,0:T(8,128)S(1)}, f32[416,128]{1,0:T(8,128)S(1)}, u32[]{:S(2)}, u32[]{:S(2)}) collective-permute-start(f32[416,128]{1,0:T(8,128)S(1)} %slice.120), channel_id=1, source_target_pairs={{0,2},{1,3},{2,4},{3,5},{4,6},{5,7},{8,10},{9,11},{10,12},{11,13},... | collective-permute-start | bytes 638984 | tf_op jit(solution)/shard_map/ppermute | solution.py:19
  27.1 4.6 %collective-permute-done.1 = f32[416,128]{1,0:T(8,128)S(1)} collective-permute-done((f32[416,128]{1,0:T(8,128)S(1)}, f32[416,128]{1,0:T(8,128)S(1)}, u32[]{:S(2)}, u32[]{:S(2)}) %collective-permute-start.1) | collective-permute-done | bytes 213024 | tf_op jit(solution)/shard_map/ppermute | solution.py:19
  36.5 2.3 collective-permute-done.3
  38.9 6.8 %collective-permute-done.5 = f32[416,128]{1,0:T(8,128)S(1)} collective-permute-done((f32[416,128]{1,0:T(8,128)}, f32[416,128]{1,0:T(8,128)S(1)}, u32[]{:S(2)}, u32[]{:S(2)}) %collective-permute-start.5) | collective-permute-done | bytes 213024 | tf_op jit(solution)/shard_map/ppermute | solution.py:19
  46.8 10.0 %all_gather.12 = f32[1024,128]{1,0:T(8,128)S(1)} all-gather(f32[256,128]{1,0:T(8,128)S(1)} %fusion.65), channel_id=1, replica_groups=mesh['series'=4,'tm'=8] {'series'}, dimensions={0}, use_global_device_ids=true | all-gather | bytes 655360 | tf_op jit(solution)/shard_map/all_gather | solution.py:72
  56.8 8.2 %fusion.10 = f32[1024,128]{1,0:T(8,128)} fusion(bf16[2048,1024]{1,0:T(8,128)(2,1)} %param.6, bf16[2048,1024]{1,0:T(8,128)(2,1)} %param.5, f32[1024,128]{1,0:T(8,128)S(1)} %all_gather.12, f32[2048,128]{1,0:T(8,128)S(1)} %copy-done), kind=kOutput, calls=%fused_computation.22 | convolution fusion | flops 1084882944 | bytes 10485760 | tf_op jit(solution)/shard_map/dot_general | solution.py:62
  66.5 4.1 %collective-permute-start.7 = (f32[416,128]{1,0:T(8,128)S(1)}, f32[416,128]{1,0:T(8,128)S(1)}, u32[]{:S(2)}, u32[]{:S(2)}) collective-permute-start(f32[416,128]{1,0:T(8,128)S(1)} %slice.156), channel_id=1, source_target_pairs={{0,2},{1,3},{2,4},{3,5},{4,6},{5,7},{8,10},{9,11},{10,12},{11,13},... | collective-permute-start | bytes 638984 | tf_op jit(solution)/shard_map/ppermute | solution.py:19
  70.6 2.8 collective-permute-start.6
  74.2 2.0 collective-permute-done.7
  80.4 2.8 collective-permute-done.9
  83.2 7.9 %collective-permute-done.11 = f32[416,128]{1,0:T(8,128)S(1)} collective-permute-done((f32[416,128]{1,0:T(8,128)S(1)}, f32[416,128]{1,0:T(8,128)S(1)}, u32[]{:S(2)}, u32[]{:S(2)}) %collective-permute-start.11) | collective-permute-done | bytes 213024 | tf_op jit(solution)/shard_map/ppermute | solution.py:19
  92.1 10.0 %all_gather.13 = f32[1024,128]{1,0:T(8,128)S(1)} all-gather(f32[256,128]{1,0:T(8,128)S(1)} %fusion.55), channel_id=1, replica_groups=mesh['series'=4,'tm'=8] {'series'}, dimensions={0}, use_global_device_ids=true | all-gather | bytes 655360 | tf_op jit(solution)/shard_map/all_gather | solution.py:72
  102.1 6.9 %fusion.7 = f32[2048,128]{1,0:T(8,128)} fusion(bf16[2048,1024]{1,0:T(8,128)(2,1)} %param.6, bf16[2048,1024]{1,0:T(8,128)(2,1)} %param.5, f32[1024,128]{1,0:T(8,128)S(1)} %all_gather.13, f32[2048,128]{1,0:T(8,128)S(1)} %copy-done), kind=kOutput, calls=%fused_computation.19 | convolution fusion | flops 1084751872 | bytes 11010048 | tf_op jit(solution)/shard_map/dot_general | solution.py:75
  109.2 57.6 %all-reduce.3.cloned.1.call-done = f32[2048,128]{1,0:T(8,128)} async-done(((f32[2048,128]{1,0:T(8,128)}), f32[2048,128]{1,0:T(8,128)}) %all-reduce.3.cloned.1.call-update) | async-done | bytes 1048592 | tf_op jit(solution)/shard_map/psum | solution.py:76
  168.3 8.2 %fusion.9 = f32[1024,128]{1,0:T(8,128)} fusion(bf16[2048,128]{1,0:T(8,128)(2,1)S(1)} %fusion.20, bf16[2048,1024]{1,0:T(8,128)(2,1)} %param.6, bf16[2048,1024]{1,0:T(8,128)(2,1)} %param.5, f32[1024,128]{1,0:T(8,128)S(1)} %all_gather.13), kind=kOutput, calls=%fused_computation.21 | convolution fusion | flops 1084358656 | bytes 9961472 | tf_op jit(solution)/shard_map/dot_general | solution.py:62
  178.0 3.2 collective-permute-start.13
  181.2 3.1 collective-permute-start.12
  190.9 2.8 collective-permute-done.15
  193.7 8.0 %collective-permute-done.17 = f32[416,128]{1,0:T(8,128)} collective-permute-done((f32[416,128]{1,0:T(8,128)S(1)}, f32[416,128]{1,0:T(8,128)}, u32[]{:S(2)}, u32[]{:S(2)}) %collective-permute-start.17) | collective-permute-done | bytes 213024 | tf_op jit(solution)/shard_map/ppermute | solution.py:19
  202.7 10.0 %all_gather.14 = f32[1024,128]{1,0:T(8,128)S(1)} all-gather(f32[256,128]{1,0:T(8,128)S(1)} %fusion.45), channel_id=1, replica_groups=mesh['series'=4,'tm'=8] {'series'}, dimensions={0}, use_global_device_ids=true | all-gather | bytes 655360 | tf_op jit(solution)/shard_map/all_gather | solution.py:72
  212.8 8.2 %fusion.8 = f32[1024,128]{1,0:T(8,128)} fusion(bf16[2048,128]{1,0:T(8,128)(2,1)S(1)} %fusion.20, bf16[2048,1024]{1,0:T(8,128)(2,1)} %param.6, bf16[2048,1024]{1,0:T(8,128)(2,1)} %param.5, f32[1024,128]{1,0:T(8,128)S(1)} %all_gather.14), kind=kOutput, calls=%fused_computation.20 | convolution fusion | flops 1084358656 | bytes 9961472 | tf_op jit(solution)/shard_map/dot_general | solution.py:62
  222.5 4.3 %collective-permute-start.19 = (f32[416,128]{1,0:T(8,128)S(1)}, f32[416,128]{1,0:T(8,128)S(1)}, u32[]{:S(2)}, u32[]{:S(2)}) collective-permute-start(f32[416,128]{1,0:T(8,128)S(1)} %slice.172), channel_id=1, source_target_pairs={{0,2},{1,3},{2,4},{3,5},{4,6},{5,7},{8,10},{9,11},{10,12},{11,13},... | collective-permute-start | bytes 638984 | tf_op jit(solution)/shard_map/ppermute | solution.py:19
  226.8 3.1 collective-permute-start.18
  236.5 2.8 collective-permute-done.21
  239.3 8.0 %collective-permute-done.23 = f32[416,128]{1,0:T(8,128)} collective-permute-done((f32[416,128]{1,0:T(8,128)S(1)}, f32[416,128]{1,0:T(8,128)}, u32[]{:S(2)}, u32[]{:S(2)}) %collective-permute-start.23) | collective-permute-done | bytes 213024 | tf_op jit(solution)/shard_map/ppermute | solution.py:19
  248.3 10.1 %all_gather.15 = f32[1024,128]{1,0:T(8,128)S(1)} all-gather(f32[256,128]{1,0:T(8,128)S(1)} %fusion.35), channel_id=1, replica_groups=mesh['series'=4,'tm'=8] {'series'}, dimensions={0}, use_global_device_ids=true | all-gather | bytes 655360 | tf_op jit(solution)/shard_map/all_gather | solution.py:72
  258.4 7.0 %fusion.6 = f32[2048,128]{1,0:T(8,128)} fusion(bf16[2048,1024]{1,0:T(8,128)(2,1)} %param.6, bf16[2048,1024]{1,0:T(8,128)(2,1)} %param.5, bf16[2048,128]{1,0:T(8,128)(2,1)S(1)} %fusion.20, f32[1024,128]{1,0:T(8,128)S(1)} %all_gather.15), kind=kOutput, calls=%fused_computation.18 | convolution fusion | flops 1084489728 | bytes 10485760 | tf_op jit(solution)/shard_map/dot_general | solution.py:75
  265.4 58.4 %all-reduce.5.cloned.1.call-done = f32[2048,128]{1,0:T(8,128)} async-done(((f32[2048,128]{1,0:T(8,128)}), f32[2048,128]{1,0:T(8,128)}) %all-reduce.5.cloned.1.call-update) | async-done | bytes 1048592 | tf_op jit(solution)/shard_map/psum | solution.py:76
  323.8 2.5 multiply_subtract_fusion
  (92 shorter events, 33.8 us)
Async XLA Ops:
  7.2 38.5 %reduce-scatter.5.cloned.1.call-start = ((), (), s32[]{:S(2)}) async-start(), calls=%async_computation.4 | async-start | bytes 655360 | tf_op jit(solution)/shard_map/reduce_scatter | solution.py:66
  16.3 40.5 %copy-start = (f32[2048,128]{1,0:T(8,128)S(1)}, f32[2048,128]{1,0:T(8,128)}, u32[]{:S(2)}) copy-start(f32[2048,128]{1,0:T(8,128)} %param.7) | copy-start | bytes 3145732
  16.3 74.7 %reduce-scatter.7.cloned.1.call-start = ((), (), s32[]{:S(2)}) async-start(), calls=%async_computation.5 | async-start | bytes 655360 | tf_op jit(solution)/shard_map/reduce_scatter | solution.py:66
  16.4 15.3 %collective-permute-start.2 = (f32[608,128]{1,0:T(8,128)S(1)}, f32[608,128]{1,0:T(8,128)S(1)}, u32[]{:S(2)}, u32[]{:S(2)}) collective-permute-start(f32[608,128]{1,0:T(8,128)S(1)} %slice.121), channel_id=1, source_target_pairs={{0,1},{1,2},{2,3},{3,4},{4,5},{5,6},{6,7},{8,9},{9,10},{10,11},{11... | collective-permute-start | bytes 933896 | tf_op jit(solution)/shard_map/ppermute | solution.py:19
  19.0 8.1 %collective-permute-start = (f32[1,128]{1,0:T(1,128)S(1)}, f32[1,128]{1,0:T(1,128)S(1)}, u32[]{:S(2)}, u32[]{:S(2)}) collective-permute-start(f32[1,128]{1,0:T(1,128)S(1)} %slice.117), channel_id=1, source_target_pairs={{0,1},{1,2},{2,3},{3,4},{4,5},{5,6},{6,7},{8,9},{9,10},{10,11},{11... | collective-permute-start | bytes 1544 | tf_op jit(solution)/shard_map/ppermute | solution.py:19
  23.6 8.2 %collective-permute-start.1 = (f32[416,128]{1,0:T(8,128)S(1)}, f32[416,128]{1,0:T(8,128)S(1)}, u32[]{:S(2)}, u32[]{:S(2)}) collective-permute-start(f32[416,128]{1,0:T(8,128)S(1)} %slice.120), channel_id=1, source_target_pairs={{0,2},{1,3},{2,4},{3,5},{4,6},{5,7},{8,10},{9,11},{10,12},{11,13},... | collective-permute-start | bytes 638984 | tf_op jit(solution)/shard_map/ppermute | solution.py:19
  31.9 13.8 %collective-permute-start.4 = (f32[608,128]{1,0:T(8,128)S(1)}, f32[608,128]{1,0:T(8,128)S(1)}, u32[]{:S(2)}, u32[]{:S(2)}) collective-permute-start(f32[608,128]{1,0:T(8,128)S(1)} %slice.152), channel_id=1, source_target_pairs={{1,0},{2,1},{3,2},{4,3},{5,4},{6,5},{7,6},{9,8},{10,9},{11,10},{12... | collective-permute-start | bytes 933896 | tf_op jit(solution)/shard_map/ppermute | solution.py:19
  33.9 11.8 %collective-permute-start.5 = (f32[416,128]{1,0:T(8,128)}, f32[416,128]{1,0:T(8,128)S(1)}, u32[]{:S(2)}, u32[]{:S(2)}) collective-permute-start(f32[416,128]{1,0:T(8,128)} %slice.153), channel_id=1, source_target_pairs={{2,0},{3,1},{4,2},{5,3},{6,4},{7,5},{10,8},{11,9},{12,10},{13,11},... | collective-permute-start | bytes 638984 | tf_op jit(solution)/shard_map/ppermute | solution.py:19
  35.2 3.7 %collective-permute-start.3 = (f32[1,128]{1,0:T(1,128)S(1)}, f32[1,128]{1,0:T(1,128)S(1)}, u32[]{:S(2)}, u32[]{:S(2)}) collective-permute-start(f32[1,128]{1,0:T(1,128)S(1)} %slice.151), channel_id=1, source_target_pairs={{1,0},{2,1},{3,2},{4,3},{5,4},{6,5},{7,6},{9,8},{10,9},{11,10},{12... | collective-permute-start | bytes 1544 | tf_op jit(solution)/shard_map/ppermute | solution.py:19
  65.1 101.8 %all-reduce.3.cloned.1.call-start = ((), (), s32[]{:S(2)}) async-start(), calls=%async_computation.6 | async-start | bytes 2097152 | tf_op jit(solution)/shard_map/psum | solution.py:76
  65.2 11.1 %collective-permute-start.8 = (f32[608,128]{1,0:T(8,128)S(1)}, f32[608,128]{1,0:T(8,128)S(1)}, u32[]{:S(2)}, u32[]{:S(2)}) collective-permute-start(f32[608,128]{1,0:T(8,128)S(1)} %slice.157), channel_id=1, source_target_pairs={{0,1},{1,2},{2,3},{3,4},{4,5},{5,6},{6,7},{8,9},{9,10},{10,11},{11... | collective-permute-start | bytes 933896 | tf_op jit(solution)/shard_map/ppermute | solution.py:19
  66.5 9.7 %collective-permute-start.7 = (f32[416,128]{1,0:T(8,128)S(1)}, f32[416,128]{1,0:T(8,128)S(1)}, u32[]{:S(2)}, u32[]{:S(2)}) collective-permute-start(f32[416,128]{1,0:T(8,128)S(1)} %slice.156), channel_id=1, source_target_pairs={{0,2},{1,3},{2,4},{3,5},{4,6},{5,7},{8,10},{9,11},{10,12},{11,13},... | collective-permute-start | bytes 638984 | tf_op jit(solution)/shard_map/ppermute | solution.py:19
  70.6 3.6 %collective-permute-start.6 = (f32[1,128]{1,0:T(1,128)S(1)}, f32[1,128]{1,0:T(1,128)S(1)}, u32[]{:S(2)}, u32[]{:S(2)}) collective-permute-start(f32[1,128]{1,0:T(1,128)S(1)} %slice.154), channel_id=1, source_target_pairs={{0,1},{1,2},{2,3},{3,4},{4,5},{5,6},{6,7},{8,9},{9,10},{10,11},{11... | collective-permute-start | bytes 1544 | tf_op jit(solution)/shard_map/ppermute | solution.py:19
  76.4 14.6 %collective-permute-start.10 = (f32[608,128]{1,0:T(8,128)S(1)}, f32[608,128]{1,0:T(8,128)S(1)}, u32[]{:S(2)}, u32[]{:S(2)}) collective-permute-start(f32[608,128]{1,0:T(8,128)S(1)} %slice.160), channel_id=1, source_target_pairs={{1,0},{2,1},{3,2},{4,3},{5,4},{6,5},{7,6},{9,8},{10,9},{11,10},{12... | collective-permute-start | bytes 933896 | tf_op jit(solution)/shard_map/ppermute | solution.py:19
  77.7 13.3 %collective-permute-start.11 = (f32[416,128]{1,0:T(8,128)S(1)}, f32[416,128]{1,0:T(8,128)S(1)}, u32[]{:S(2)}, u32[]{:S(2)}) collective-permute-start(f32[416,128]{1,0:T(8,128)S(1)} %slice.161), channel_id=1, source_target_pairs={{2,0},{3,1},{4,2},{5,3},{6,4},{7,5},{10,8},{11,9},{12,10},{13,11},... | collective-permute-start | bytes 638984 | tf_op jit(solution)/shard_map/ppermute | solution.py:19
  79.0 4.2 %collective-permute-start.9 = (f32[1,128]{1,0:T(1,128)S(1)}, f32[1,128]{1,0:T(1,128)S(1)}, u32[]{:S(2)}, u32[]{:S(2)}) collective-permute-start(f32[1,128]{1,0:T(1,128)S(1)} %slice.159), channel_id=1, source_target_pairs={{1,0},{2,1},{3,2},{4,3},{5,4},{6,5},{7,6},{9,8},{10,9},{11,10},{12... | collective-permute-start | bytes 1544 | tf_op jit(solution)/shard_map/ppermute | solution.py:19
  109.0 92.7 %reduce-scatter.9.cloned.1.call-start = ((), (), s32[]{:S(2)}) async-start(), calls=%async_computation.7 | async-start | bytes 655360 | tf_op jit(solution)/shard_map/reduce_scatter | solution.py:66
  176.6 70.7 %reduce-scatter.11.cloned.1.call-start = ((), (), s32[]{:S(2)}) async-start(), calls=%async_computation.8 | async-start | bytes 655360 | tf_op jit(solution)/shard_map/reduce_scatter | solution.py:66
  176.6 10.1 %collective-permute-start.14 = (f32[608,128]{1,0:T(8,128)S(1)}, f32[608,128]{1,0:T(8,128)S(1)}, u32[]{:S(2)}, u32[]{:S(2)}) collective-permute-start(f32[608,128]{1,0:T(8,128)S(1)} %slice.165), channel_id=1, source_target_pairs={{0,1},{1,2},{2,3},{3,4},{4,5},{5,6},{6,7},{8,9},{9,10},{10,11},{11... | collective-permute-start | bytes 933896 | tf_op jit(solution)/shard_map/ppermute | solution.py:19
  178.0 8.8 %collective-permute-start.13 = (f32[416,128]{1,0:T(8,128)S(1)}, f32[416,128]{1,0:T(8,128)S(1)}, u32[]{:S(2)}, u32[]{:S(2)}) collective-permute-start(f32[416,128]{1,0:T(8,128)S(1)} %slice.164), channel_id=1, source_target_pairs={{0,2},{1,3},{2,4},{3,5},{4,6},{5,7},{8,10},{9,11},{10,12},{11,13},... | collective-permute-start | bytes 638984 | tf_op jit(solution)/shard_map/ppermute | solution.py:19
  181.2 3.9 %collective-permute-start.12 = (f32[1,128]{1,0:T(1,128)S(1)}, f32[1,128]{1,0:T(1,128)S(1)}, u32[]{:S(2)}, u32[]{:S(2)}) collective-permute-start(f32[1,128]{1,0:T(1,128)S(1)} %slice.162), channel_id=1, source_target_pairs={{0,1},{1,2},{2,3},{3,4},{4,5},{5,6},{6,7},{8,9},{9,10},{10,11},{11... | collective-permute-start | bytes 1544 | tf_op jit(solution)/shard_map/ppermute | solution.py:19
  186.9 14.8 %collective-permute-start.16 = (f32[608,128]{1,0:T(8,128)S(1)}, f32[608,128]{1,0:T(8,128)S(1)}, u32[]{:S(2)}, u32[]{:S(2)}) collective-permute-start(f32[608,128]{1,0:T(8,128)S(1)} %slice.168), channel_id=1, source_target_pairs={{1,0},{2,1},{3,2},{4,3},{5,4},{6,5},{7,6},{9,8},{10,9},{11,10},{12... | collective-permute-start | bytes 933896 | tf_op jit(solution)/shard_map/ppermute | solution.py:19
  188.2 13.4 %collective-permute-start.17 = (f32[416,128]{1,0:T(8,128)S(1)}, f32[416,128]{1,0:T(8,128)}, u32[]{:S(2)}, u32[]{:S(2)}) collective-permute-start(f32[416,128]{1,0:T(8,128)S(1)} %slice.169), channel_id=1, source_target_pairs={{2,0},{3,1},{4,2},{5,3},{6,4},{7,5},{10,8},{11,9},{12,10},{13,11},... | collective-permute-start | bytes 638984 | tf_op jit(solution)/shard_map/ppermute | solution.py:19
  189.6 4.2 %collective-permute-start.15 = (f32[1,128]{1,0:T(1,128)S(1)}, f32[1,128]{1,0:T(1,128)S(1)}, u32[]{:S(2)}, u32[]{:S(2)}) collective-permute-start(f32[1,128]{1,0:T(1,128)S(1)} %slice.167), channel_id=1, source_target_pairs={{1,0},{2,1},{3,2},{4,3},{5,4},{6,5},{7,6},{9,8},{10,9},{11,10},{12... | collective-permute-start | bytes 1544 | tf_op jit(solution)/shard_map/ppermute | solution.py:19
  221.0 102.7 %all-reduce.5.cloned.1.call-start = ((), (), s32[]{:S(2)}) async-start(), calls=%async_computation.9 | async-start | bytes 2097152 | tf_op jit(solution)/shard_map/psum | solution.py:76
  221.1 11.3 %collective-permute-start.20 = (f32[608,128]{1,0:T(8,128)S(1)}, f32[608,128]{1,0:T(8,128)S(1)}, u32[]{:S(2)}, u32[]{:S(2)}) collective-permute-start(f32[608,128]{1,0:T(8,128)S(1)} %slice.173), channel_id=1, source_target_pairs={{0,1},{1,2},{2,3},{3,4},{4,5},{5,6},{6,7},{8,9},{9,10},{10,11},{11... | collective-permute-start | bytes 933896 | tf_op jit(solution)/shard_map/ppermute | solution.py:19
  222.5 9.9 %collective-permute-start.19 = (f32[416,128]{1,0:T(8,128)S(1)}, f32[416,128]{1,0:T(8,128)S(1)}, u32[]{:S(2)}, u32[]{:S(2)}) collective-permute-start(f32[416,128]{1,0:T(8,128)S(1)} %slice.172), channel_id=1, source_target_pairs={{0,2},{1,3},{2,4},{3,5},{4,6},{5,7},{8,10},{9,11},{10,12},{11,13},... | collective-permute-start | bytes 638984 | tf_op jit(solution)/shard_map/ppermute | solution.py:19
  226.8 3.9 %collective-permute-start.18 = (f32[1,128]{1,0:T(1,128)S(1)}, f32[1,128]{1,0:T(1,128)S(1)}, u32[]{:S(2)}, u32[]{:S(2)}) collective-permute-start(f32[1,128]{1,0:T(1,128)S(1)} %slice.170), channel_id=1, source_target_pairs={{0,1},{1,2},{2,3},{3,4},{4,5},{5,6},{6,7},{8,9},{9,10},{10,11},{11... | collective-permute-start | bytes 1544 | tf_op jit(solution)/shard_map/ppermute | solution.py:19
  232.5 14.8 %collective-permute-start.22 = (f32[608,128]{1,0:T(8,128)S(1)}, f32[608,128]{1,0:T(8,128)S(1)}, u32[]{:S(2)}, u32[]{:S(2)}) collective-permute-start(f32[608,128]{1,0:T(8,128)S(1)} %slice.176), channel_id=1, source_target_pairs={{1,0},{2,1},{3,2},{4,3},{5,4},{6,5},{7,6},{9,8},{10,9},{11,10},{12... | collective-permute-start | bytes 933896 | tf_op jit(solution)/shard_map/ppermute | solution.py:19
  233.9 13.4 %collective-permute-start.23 = (f32[416,128]{1,0:T(8,128)S(1)}, f32[416,128]{1,0:T(8,128)}, u32[]{:S(2)}, u32[]{:S(2)}) collective-permute-start(f32[416,128]{1,0:T(8,128)S(1)} %slice.177), channel_id=1, source_target_pairs={{2,0},{3,1},{4,2},{5,3},{6,4},{7,5},{10,8},{11,9},{12,10},{13,11},... | collective-permute-start | bytes 638984 | tf_op jit(solution)/shard_map/ppermute | solution.py:19
  235.2 4.2 %collective-permute-start.21 = (f32[1,128]{1,0:T(1,128)S(1)}, f32[1,128]{1,0:T(1,128)S(1)}, u32[]{:S(2)}, u32[]{:S(2)}) collective-permute-start(f32[1,128]{1,0:T(1,128)S(1)} %slice.175), channel_id=1, source_target_pairs={{1,0},{2,1},{3,2},{4,3},{5,4},{6,5},{7,6},{9,8},{10,9},{11,10},{12... | collective-permute-start | bytes 1544 | tf_op jit(solution)/shard_map/ppermute | solution.py:19
  258.4 65.4 %copy-start.2 = (f32[2048,128]{1,0:T(8,128)S(1)}, f32[2048,128]{1,0:T(8,128)}, u32[]{:S(2)}) copy-start(f32[2048,128]{1,0:T(8,128)} %all-reduce.3.cloned.1.call-done) | copy-start | bytes 3145732
  (2 other events, 29.1 us)
Sparse Core Ops, SparseCore 0:
  16.4 27.8 reduce-scatter.4
  65.2 23.8 reduce-scatter.6
  109.1 57.7 all-reduce.2
  176.7 24.1 reduce-scatter.8
  221.2 24.5 reduce-scatter.10
  265.5 58.2 all-reduce.4
where the time goes:
time: 335 us; the launch traced here: 334 us
  waiting for transfers between devices  170 us (51%)
  starting transfers between devices  51 us (15%)
  matrix products  47.7 us (14%)
  blocking collectives  40.2 us (12%)
  between operations  14.6 us (4%)
  other arithmetic  8.5 us (3%)
    psum x2, waiting for transfers between devices, body(): grad_f = lax.psum(partial_load, 'tm')  116 us
    ppermute x24, waiting for transfers between devices, shifted(): lax.ppermute(value, axis, [(source, source + steps) for source in range(i...  53.9 us
    ppermute x24, starting transfers between devices, shifted(): lax.ppermute(value, axis, [(source, source + steps) for source in range(i...  50.6 us
    all_gather x4, blocking collectives, body(): times = lax.all_gather(updated, 'series', axis=0, tiled=True)  40.2 us
    dot_general x4, matrix products, body(): lax.dot_general(rb, fb, (((0,), (0,)), ((), ())), preferred_element_type=...  33.8 us
    dot_general x2, matrix products, body(): partial_load = jnp.dot(rb, xb, preferred_element_type=jnp.float32)  13.9 us
  transfers between devices with their start and end apart: 30, of which 17 were waited for; matrix products, arithmetic and copies ran while one was open for 0% of the time, Pallas kernels for 0%

commit v1 on v0

v1 whole, which is shorter than its diff:
```python
import jax
import jax.numpy as jnp
from jax import lax
from jax.experimental import pallas as pl
from jax.experimental.pallas import tpu as pltpu
from jax.sharding import PartitionSpec as P

LAG = 1440
OUTER = 2
TIME_STEPS = 2

smooth = 4.0
shrink = 0.1
margin = 32.0
hidden = 64.0
PAD = 8
F32 = jnp.float32
BF16 = jnp.bfloat16
VMEM = pl.BlockSpec(memory_space=pltpu.VMEM)
ANY = pl.BlockSpec(memory_space=pl.ANY)


def dot_nt(a, b):
    return lax.dot_general(a, b, (((1,), (1,)), ((), ())), preferred_element_type=F32)


def dot_tn(a, b):
    return lax.dot_general(a, b, (((0,), (0,)), ((), ())), preferred_element_type=F32)


def dot_nn(a, b):
    return lax.dot_general(a, b, (((1,), (0,)), ((), ())), preferred_element_type=F32)


def up8(value):
    return -(-value // 8) * 8


class Plan:
    def __init__(self, n_s, n_t, series, minutes, rank):
        self.n_s, self.n_t, self.series, self.minutes, self.rank = n_s, n_t, series, minutes, rank
        self.rows = minutes // n_s
        self.n_z = n_t // 2
        self.block = series // n_t
        self.half = series // 2
        need = []
        for s in range(n_s):
            first = s * self.rows
            by_delta = {}
            spans = [("back", first - LAG, self.rows + 1), ("far", first + LAG - 1, self.rows + 1)]
            if s == 0:
                spans.append(("prev", -1, 1))
            if s == n_s - 1:
                spans.append(("next", minutes, 1))
            for kind, row, count in spans:
                at = 0
                while at < count:
                    delta = (row + at) // minutes
                    local = (row + at) % minutes
                    size = min(count - at, minutes - local)
                    assert delta != 0
                    by_delta.setdefault(delta, []).append((kind, at, local, size))
                    at += size
            order = sorted(by_delta.items(), key=lambda item: (-sum(p[3] for p in item[1]), item[0]))
            need.append(order)
        self.slots = max(len(order) for order in need)
        self.pieces = []
        self.length = []
        self.pairs = []
        for slot in range(self.slots):
            per_s, pairs, length = [], [], 8
            for s in range(n_s):
                placed, offset = [], 0
                if slot < len(need[s]):
                    delta, parts = need[s][slot]
                    for kind, at, local, size in parts:
                        placed.append((kind, at, local, size, offset))
                        offset += up8(size)
                    for t in range(n_t):
                        if 0 <= t + delta < n_t:
                            pairs.append((s * n_t + t + delta, s * n_t + t))
                length = max(length, offset)
                per_s.append(placed)
            self.pieces.append(per_s)
            self.length.append(length)
            self.pairs.append(pairs)


def load_x(plan, x_refs, xs):
    s = lax.axis_index("series")
    rows = plan.rows
    if len(x_refs) == 1:
        xs[pl.ds(PAD, plan.minutes), :] = x_refs[0][...]
    else:
        for k in range(plan.n_s):
            start = pl.multiple_of(PAD + jnp.bitwise_xor(s, k) * rows, 8)
            xs[pl.ds(start, rows), :] = x_refs[k][...]


def pack_halo(plan, xs, h_refs, win):
    s = lax.axis_index("series")
    start = pl.multiple_of(s * plan.rows, 8)
    win[...] = xs[pl.ds(start, plan.rows + 2 * PAD), :]
    for value in range(plan.n_s):
        @pl.when(s == value)
        def _():
            for slot in range(plan.slots):
                for kind, at, local, size, offset in plan.pieces[slot][value]:
                    h_refs[slot][pl.ds(offset, size), :] = xs[pl.ds(PAD + local, size), :]


def residual(prod, obs):
    obs = obs.astype(F32)
    return jnp.where(obs < 0.5 * hidden, prod - obs, 0.0).astype(BF16)


def halo_shapes(plan):
    shapes = [jax.ShapeDtypeStruct((length, plan.rank), F32) for length in plan.length]
    return shapes + [jax.ShapeDtypeStruct((plan.rows + 2 * PAD, plan.rank), F32)]


def time_pass(plan, data, loads, xp, halo):
    first = len(data) == 2
    n_s, rows, series, minutes, rank = plan.n_s, plan.rows, plan.series, plan.minutes, plan.rank
    chunk = series // 4
    count = series // chunk
    n_x = len(xp)
    n_h = plan.slots + 1 if halo else 0

    def kernel(*refs):
        refs = list(refs)
        d_refs = [refs.pop(0) for _ in data]
        f = refs.pop(0)
        x_refs = [refs.pop(0) for _ in range(n_x)]
        g_refs = [refs.pop(0) for _ in range(n_s)]
        h_refs = [refs.pop(0) for _ in range(n_h)]
        packed = refs.pop(0) if first else None
        bufs = [refs.pop(0) for _ in data]
        xs, acc, sem = refs
        copies = []
        for c in range(count):
            span = pl.ds(c * chunk, chunk)
            copies.append([pltpu.make_async_copy(d.at[span, :], b.at[span, :], sem.at[i, c])
                           for i, (d, b) in enumerate(zip(d_refs, bufs))])
        for group in copies:
            for copy in group:
                copy.start()
        load_x(plan, x_refs, xs)
        if halo:
            pack_halo(plan, xs, h_refs[:-1], h_refs[-1])
        xb = xs[pl.ds(PAD, minutes), :].astype(BF16)
        outs = []
        for c in range(count):
            span = pl.ds(c * chunk, chunk)
            for copy in copies[c]:
                copy.wait()
            if first:
                kept = jnp.where(bufs[1][span, :] > 0, bufs[0][span, :], jnp.full((), hidden, BF16))
                bufs[0][span, :] = kept
                out = pltpu.make_async_copy(bufs[0].at[span, :], packed.at[span, :], sem.at[2, c])
                out.start()
                outs.append(out)
            fb = f[span, :].astype(BF16)
            part = dot_tn(fb, residual(dot_nt(fb, xb), bufs[0][span, :]))
            if c == 0:
                acc[...] = part
            else:
                acc[...] += part
        s = lax.axis_index("series")
        for k in range(n_s):
            start = pl.multiple_of(jnp.bitwise_xor(s, k) * rows, 128)
            g_refs[k][...] = acc[:, pl.ds(start, rows)].T
        for out in outs:
            out.wait()

    out_shape = [jax.ShapeDtypeStruct((rows, rank), F32) for _ in range(n_s)]
    out_specs = [VMEM] * n_s
    if halo:
        out_shape += halo_shapes(plan)
        out_specs += [VMEM] * n_h
    if first:
        out_shape.append(jax.ShapeDtypeStruct((series, minutes), BF16))
        out_specs.append(ANY)
    outs = pl.pallas_call(
        kernel,
        in_specs=[ANY] * len(data) + [VMEM] * (1 + n_x),
        out_specs=out_specs,
        out_shape=out_shape,
        scratch_shapes=[pltpu.VMEM((series, minutes), BF16) for _ in data]
        + [pltpu.VMEM((minutes + 2 * PAD, rank), F32), pltpu.VMEM((rank, minutes), F32),
           pltpu.SemaphoreType.DMA((3, count))],
        name="time_pass",
    )(*data, loads, *xp)
    outs = list(outs)
    grads = outs[:n_s]
    halos = outs[n_s:n_s + n_h]
    return grads, halos, (outs[-1] if first else None)


def load_pass(plan, data, loads, xp, halo):
    n_s, series, minutes, rank = plan.n_s, plan.series, plan.minutes, plan.rank
    block, n_z, half = plan.block, plan.n_z, plan.half
    n_x = len(xp)
    n_h = plan.slots + 1 if halo else 1
    count = 2 * n_z

    def kernel(*refs):
        refs = list(refs)
        d = refs.pop(0)
        f = refs.pop(0)
        x_refs = [refs.pop(0) for _ in range(n_x)]
        other = refs.pop(0)
        mine = [refs.pop(0) for _ in range(n_z)]
        h_refs = [refs.pop(0) for _ in range(n_h)]
        buf, xs, sem = refs
        t = lax.axis_index("tm")
        core, z = t % 2, t // 2
        spans, copies = [], []
        for c in range(count):
            side = core if c >= n_z else 1 - core
            start = pl.multiple_of(side * half + jnp.bitwise_xor(z, c % n_z) * block, block)
            spans.append(pl.ds(start, block))
            copies.append(pltpu.make_async_copy(d.at[spans[c], :], buf.at[pl.ds(c * block, block), :], sem.at[c]))
        for copy in copies:
            copy.start()
        load_x(plan, x_refs, xs)
        xb = xs[pl.ds(PAD, minutes), :].astype(BF16)
        for c in range(count):
            copies[c].wait()
            fb = f[spans[c], :].astype(BF16)
            rb = residual(dot_nt(fb, xb), buf[pl.ds(c * block, block), :])
            part = dot_nn(rb, xb)
            if c < n_z:
                other[pl.ds(c * block, block), :] = part
            else:
                mine[c - n_z][...] = part
        if halo:
            pack_halo(plan, xs, h_refs[:-1], h_refs[-1])
        else:
            h_refs[0][...] = xs[pl.ds(PAD, minutes), :]

    out_shape = [jax.ShapeDtypeStruct((half, rank), F32)]
    out_shape += [jax.ShapeDtypeStruct((block, rank), F32) for _ in range(n_z)]
    out_shape += halo_shapes(plan) if halo else [jax.ShapeDtypeStruct((minutes, rank), F32)]
    outs = pl.pallas_call(
        kernel,
        in_specs=[ANY] + [VMEM] * (1 + n_x),
        out_specs=[VMEM] * len(out_shape),
        out_shape=out_shape,
        scratch_shapes=[pltpu.VMEM((series, minutes), BF16), pltpu.VMEM((minutes + 2 * PAD, rank), F32),
                        pltpu.SemaphoreType.DMA((count,))],
        name="load_pass",
    )(data, loads, *xp)
    outs = list(outs)
    return outs[0], outs[1:1 + n_z], outs[1 + n_z:]


def smoothing(plan, win, halos, lag_weights):
    rows, rank = plan.rows, plan.rank
    total = plan.minutes * plan.n_t

    def kernel(*refs):
        refs = list(refs)
        win_ref = refs.pop(0)
        h_refs = [refs.pop(0) for _ in range(plan.slots)]
        w_ref, out, xw, far, near = refs
        s = lax.axis_index("series")
        t = lax.axis_index("tm")
        xw[...] = win_ref[...]
        for value in range(plan.n_s):
            @pl.when(s == value)
            def _():
                for slot in range(plan.slots):
                    for kind, at, local, size, offset in plan.pieces[slot][value]:
                        target, place = {"back": (near, at), "far": (far, at),
                                         "prev": (xw, PAD - 1), "next": (xw, PAD + rows)}[kind]
                        target[pl.ds(place, size), :] = h_refs[slot][pl.ds(offset, size), :]
        w0 = w_ref[0:1, :]
        w1 = w_ref[1:2, :]
        x = xw[pl.ds(PAD, rows), :]
        here = t * plan.minutes + s * rows + lax.broadcasted_iota(jnp.int32, (rows, rank), 0)
        resid = x - w0 * xw[pl.ds(PAD - 1, rows), :] - w1 * near[pl.ds(0, rows), :]
        after_one = xw[pl.ds(PAD + 1, rows), :] - w0 * x - w1 * near[pl.ds(1, rows), :]
        after_far = far[pl.ds(1, rows), :] - w0 * far[pl.ds(0, rows), :] - w1 * x
        after_one = jnp.where(here + 1 < total, after_one, 0.0)
        after_far = jnp.where(here + LAG < total, after_far, 0.0)
        out[...] = smooth * (resid - w0 * after_one - w1 * after_far)

    return pl.pallas_call(
        kernel,
        in_specs=[VMEM] * (2 + plan.slots),
        out_specs=VMEM,
        out_shape=jax.ShapeDtypeStruct((rows, rank), F32),
        scratch_shapes=[pltpu.VMEM((rows + 2 * PAD, rank), F32), pltpu.VMEM((up8(rows + 1), rank), F32),
                        pltpu.VMEM((up8(rows + 1), rank), F32)],
        name="smoothing",
    )(win, *halos, lag_weights)


def assemble(plan, mine, other):
    def kernel(*refs):
        blocks, (full, low) = refs[:2 * plan.n_z], refs[2 * plan.n_z:]
        t = lax.axis_index("tm")
        core, z = t % 2, t // 2
        for c in range(2 * plan.n_z):
            side = core if c < plan.n_z else 1 - core
            start = side * plan.half + jnp.bitwise_xor(z, c % plan.n_z) * plan.block
            span = pl.ds(pl.multiple_of(start, plan.block), plan.block)
            value = blocks[c][...]
            full[span, :] = value
            low[span, :] = value.astype(BF16)

    shape = (plan.series, plan.rank)
    return pl.pallas_call(
        kernel,
        in_specs=[VMEM] * (2 * plan.n_z),
        out_specs=[VMEM, VMEM],
        out_shape=[jax.ShapeDtypeStruct(shape, F32), jax.ShapeDtypeStruct(shape, BF16)],
        name="assemble",
    )(*mine, *other)


def body(observed, mask, loadings, factors, lag_weights):
    n_s, n_t = lax.axis_size("series"), lax.axis_size("tm")
    plan = Plan(n_s, n_t, loadings.shape[0], factors.shape[0], loadings.shape[1])
    step_time = 1.0 / (plan.series * n_s / plan.rank + margin)
    step_load = 1.0 / (plan.minutes * n_t)
    rows, n_z, block = plan.rows, plan.n_z, plan.block

    def swap(value, axis, count, k):
        return lax.ppermute(value, axis, [(i, i ^ k) for i in range(count)])

    t = lax.axis_index("tm")
    own_start = (t % 2) * plan.half + (t // 2) * block
    own_loads = lax.dynamic_slice_in_dim(loadings, own_start, block, 0)
    loads = loadings
    data = (observed, mask)
    xp = [factors]
    halos = None
    for outer in range(OUTER):
        for inner in range(TIME_STEPS):
            grads, made, packed = time_pass(plan, data, loads, xp, halos is None)
            if packed is not None:
                data = (packed,)
            if halos is None:
                halos = made
            got = [swap(grads[k], "series", n_s, k) for k in range(1, n_s)]
            sent = [lax.ppermute(h, ("series", "tm"), pairs) for h, pairs in zip(halos[:-1], plan.pairs)]
            win = halos[-1]
            smooth_grad = smoothing(plan, win, sent, lag_weights)
            share = grads[0]
            for value in got:
                share = share + value
            own = win[PAD:PAD + rows] - step_time * (share + smooth_grad)
            xp = [own] + [swap(own, "series", n_s, k) for k in range(1, n_s)]
            halos = None
        other, mine, made = load_pass(plan, data[0], loads, xp, outer + 1 < OUTER)
        halos = made
        crossed = swap(other, "tm", n_t, 1)
        mine = [m + crossed[k * block:(k + 1) * block] for k, m in enumerate(mine)]
        total = mine[0]
        for k in range(1, n_z):
            total = total + swap(mine[k], "tm", n_t, 2 * k)
        own_loads = own_loads - step_load * (total + shrink * own_loads)
        near = [own_loads] + [swap(own_loads, "tm", n_t, 2 * k) for k in range(1, n_z)]
        far = [swap(value, "tm", n_t, 1) for value in near]
        full, loads = assemble(plan, near, far)
    return (full, made[0])


def solution(mesh):
    in_specs = (P("series", "tm"), P("series", "tm"), P("series", None), P("tm", None), P())
    out_specs = (P("series", None), P("tm", None))
    return jax.shard_map(body, mesh=mesh, in_specs=in_specs, out_specs=out_specs, check_vma=False)
```

time: 335 us -> 230 us (0.69)
  waiting for transfers between devices: 170 us -> 76 us
  Pallas kernels: 0 us -> 51.5 us
  matrix products: 47.7 us -> 0 us
  blocking collectives: 40.2 us -> 0 us
  starting transfers between devices: 51 us -> 82.4 us
  between operations: 14.6 us -> 1.21 us
  local copies, waits for them, and re-layouts: 1.97 us -> 9.29 us
    psum x2 -> x0, waiting for transfers between devices: 116 us -> none  [body(): grad_f = lax.psum(partial_load, 'tm')]
    pallas_call x0 -> x12, Pallas kernels: none -> 51.5 us  [the longest x4 25 us: time_pass(): pl.pallas_call(kernel, in_specs=[ANY] * len(data) + [VMEM] * (1 + n_x), o...]
    dot_general x6 -> x0, matrix products: 47.7 us -> none  [the longest x4 33.8 us: body(): lax.dot_general(rb, fb, (((0,), (0,)), ((), ())), preferred_element_type=...]
    all_gather x4 -> x0, blocking collectives: 40.2 us -> none  [body(): times = lax.all_gather(updated, 'series', axis=0, tiled=True)]
    ppermute x24 -> x58, starting transfers between devices: 50.6 us -> 82.4 us  [the longest x46 54 us: swap(): return lax.ppermute(value, axis, [(i, i ^ k) for i in range(count)])]
    ppermute x24 -> x58, waiting for transfers between devices: 53.9 us -> 76 us  [the longest x46 76 us: swap(): return lax.ppermute(value, axis, [(i, i ^ k) for i in range(count)])]
    unnamed x9 -> x92, local copies, waits for them, and re-layouts: 0.81 us -> 9.29 us
    sub x9 -> x6, other arithmetic: 7.09 us -> 6.27 us  [the longest x4 4.29 us: body(): own = win[PAD:PAD + rows] - step_time * (share + smooth_grad)]
  transfers between devices with their start and end apart: 30 -> 58, of which waited for: 17 -> 30; matrix products, arithmetic and copies ran while one was open for 0% -> 0% of each run, Pallas kernels for 0% -> 7%
where the time goes in v1:
time: 230 us; the launch traced here: 229 us
  starting transfers between devices  82.4 us (36%)
  waiting for transfers between devices  76 us (33%)
  Pallas kernels  51.5 us (22%)
  local copies, waits for them, and re-layouts  9.29 us (4%)
  other arithmetic  8.44 us (4%)
    ppermute x46, waiting for transfers between devices, swap(): return lax.ppermute(value, axis, [(i, i ^ k) for i in range(count)])  76 us
    ppermute x46, starting transfers between devices, swap(): return lax.ppermute(value, axis, [(i, i ^ k) for i in range(count)])  54 us
    ppermute x12, starting transfers between devices, body(): lax.ppermute(h, ('series', 'tm'), pairs)  28.4 us
    pallas_call x4, Pallas kernels, time_pass(): pl.pallas_call(kernel, in_specs=[ANY] * len(data) + [VMEM] * (1 + n_x), o...  25 us
    pallas_call x2, Pallas kernels, load_pass(): pl.pallas_call(kernel, in_specs=[ANY] + [VMEM] * (1 + n_x), out_specs=[VM...  13.8 us
    unnamed x92, local copies, waits for them, and re-layouts  9.29 us
    pallas_call x4, Pallas kernels, smoothing(): pl.pallas_call(kernel, in_specs=[VMEM] * (2 + plan.slots), out_specs=VMEM...  7.48 us
    pallas_call x2, Pallas kernels, assemble(): pl.pallas_call(kernel, in_specs=[VMEM] * (2 * plan.n_z), out_specs=[VMEM,...  5.15 us
  transfers between devices with their start and end apart: 58, of which 30 were waited for; matrix products, arithmetic and copies ran while one was open for 0% of the time, Pallas kernels for 7%

profile of v1, /device:TPU:0, one launch (start us, length us, event | category | flops | bytes accessed | tf_op | source)
XLA Modules:
  0.0 228.8 jit_solution(8556352093360060100)
XLA Ops:
  0.6 7.9 %time_pass.4 = (f32[256,128]{1,0:T(8,128)}, f32[256,128]{1,0:T(8,128)}, f32[256,128]{1,0:T(8,128)}, f32[256,128]{1,0:T(8,128)}, f32[264,128]{1,0:T(8,128)}, /*in...) custom-call(bf16[2048,1024]{1,0:T(8,128)(2,1)} %refs_0_.1, ...), custom_call_target="tpu_custom_call" | custom-call | tf_op jit(solution)/shard_map/time_pass/pallas_call | solution.py:184
  10.9 4.5 %collective-permute-start.3 = (f32[264,128]{1,0:T(8,128)}, f32[264,128]{1,0:T(8,128)S(1)}, u32[]{:S(2)}, u32[]{:S(2)}) collective-permute-start(f32[264,128]{1,0:T(8,128)} %get-tuple-element.54), channel_id=1, source_target_pairs={{0,2},{1,3},{2,4},{3,5},{4,6},{5,7},{9,8},{10,9},{11,10},{12,11},{... | collective-permute-start | bytes 405512 | tf_op jit(solution)/shard_map/ppermute | solution.py:348
  16.7 3.9 %collective-permute-start = (f32[256,128]{1,0:T(8,128)}, f32[256,128]{1,0:T(8,128)S(1)}, u32[]{:S(2)}, u32[]{:S(2)}) collective-permute-start(f32[256,128]{1,0:T(8,128)} %get-tuple-element.51), channel_id=1, source_target_pairs={{0,8},{8,0},{16,24},{24,16},{1,9},{9,1},{17,25},{25,17},{2,10},{10... | collective-permute-start | bytes 393224 | tf_op jit(solution)/shard_map/ppermute | solution.py:331
  24.8 3.6 %collective-permute-done.1 = f32[256,128]{1,0:T(8,128)S(1)} collective-permute-done((f32[256,128]{1,0:T(8,128)}, f32[256,128]{1,0:T(8,128)S(1)}, u32[]{:S(2)}, u32[]{:S(2)}) %collective-permute-start.1) | collective-permute-done | bytes 131104 | tf_op jit(solution)/shard_map/ppermute | solution.py:331
  33.1 3.3 %collective-permute-done.8.refs_5_ = f32[256,128]{1,0:T(8,128)S(1)} collective-permute-done((f32[256,128]{1,0:T(8,128)S(1)}, f32[256,128]{1,0:T(8,128)S(1)}, u32[]{:S(2)}, u32[]{:S(2)}) %collective-permute-start.8) | collective-permute-done | bytes 131104 | tf_op jit(solution)/shard_map/ppermute | solution.py:331
  38.2 5.9 %time_pass.5 = (f32[256,128]{1,0:T(8,128)}, f32[256,128]{1,0:T(8,128)}, f32[256,128]{1,0:T(8,128)}, f32[256,128]{1,0:T(8,128)}, f32[264,128]{1,0:T(8,128)}, /*in...) custom-call(bf16[2048,1024]{1,0:T(8,128)(2,1)} %get-tuple-element.48.refs_0_, f32[2048,128]{1,0:T(8,128)} %refs_1_.5, ...), custom_call_target="tpu_custom_call" | custom-call | tf_op jit(solution)/shard_map/time_pass/pallas_call | solution.py:184
  45.4 3.8 %collective-permute-start.12 = (f32[264,128]{1,0:T(8,128)}, f32[264,128]{1,0:T(8,128)S(1)}, u32[]{:S(2)}, u32[]{:S(2)}) collective-permute-start(f32[264,128]{1,0:T(8,128)} %get-tuple-element.62), channel_id=1, source_target_pairs={{0,2},{1,3},{2,4},{3,5},{4,6},{5,7},{9,8},{10,9},{11,10},{12,11},{... | collective-permute-start | bytes 405512 | tf_op jit(solution)/shard_map/ppermute | solution.py:348
  50.4 3.3 %collective-permute-start.9 = (f32[256,128]{1,0:T(8,128)}, f32[256,128]{1,0:T(8,128)S(1)}, u32[]{:S(2)}, u32[]{:S(2)}) collective-permute-start(f32[256,128]{1,0:T(8,128)} %get-tuple-element.59), channel_id=1, source_target_pairs={{0,8},{8,0},{16,24},{24,16},{1,9},{9,1},{17,25},{25,17},{2,10},{10... | collective-permute-start | bytes 393224 | tf_op jit(solution)/shard_map/ppermute | solution.py:331
  58.3 3.3 %collective-permute-done.10 = f32[256,128]{1,0:T(8,128)S(1)} collective-permute-done((f32[256,128]{1,0:T(8,128)}, f32[256,128]{1,0:T(8,128)S(1)}, u32[]{:S(2)}, u32[]{:S(2)}) %collective-permute-start.10) | collective-permute-done | bytes 131104 | tf_op jit(solution)/shard_map/ppermute | solution.py:331
  66.3 3.3 %collective-permute-done.17.refs_5_ = f32[256,128]{1,0:T(8,128)S(1)} collective-permute-done((f32[256,128]{1,0:T(8,128)S(1)}, f32[256,128]{1,0:T(8,128)S(1)}, u32[]{:S(2)}, u32[]{:S(2)}) %collective-permute-start.17) | collective-permute-done | bytes 131104 | tf_op jit(solution)/shard_map/ppermute | solution.py:331
  72.2 7.2 %load_pass.2 = (f32[1024,128]{1,0:T(8,128)}, f32[256,128]{1,0:T(8,128)}, f32[256,128]{1,0:T(8,128)}, f32[256,128]{1,0:T(8,128)}, f32[256,128]{1,0:T(8,128)}, /*i...) custom-call(bf16[2048,1024]{1,0:T(8,128)(2,1)} %get-tuple-element.48.refs_0_, ...), custom_call_target="tpu_custom_call" | custom-call | tf_op jit(solution)/shard_map/load_pass/pallas_call | solution.py:245
  82.7 2.7 %collective-permute-start.19 = (f32[256,128]{1,0:T(8,128)S(1)}, f32[256,128]{1,0:T(8,128)S(1)}, u32[]{:S(2)}, u32[]{:S(2)}) collective-permute-start(f32[256,128]{1,0:T(8,128)S(1)} %get-tuple-element.97), channel_id=1, source_target_pairs={{0,2},{1,3},{2,0},{3,1},{4,6},{5,7},{6,4},{7,5},{8,10},{9,11},{10,... | collective-permute-start | bytes 393224 | tf_op jit(solution)/shard_map/ppermute | solution.py:331
  89.3 4.3 %collective-permute-done.21 = f32[256,128]{1,0:T(8,128)S(1)} collective-permute-done((f32[256,128]{1,0:T(8,128)S(1)}, f32[256,128]{1,0:T(8,128)S(1)}, u32[]{:S(2)}, u32[]{:S(2)}) %collective-permute-start.21) | collective-permute-done | bytes 131104 | tf_op jit(solution)/shard_map/ppermute | solution.py:331
  93.6 5.3 %collective-permute-done.20 = f32[256,128]{1,0:T(8,128)S(1)} collective-permute-done((f32[256,128]{1,0:T(8,128)S(1)}, f32[256,128]{1,0:T(8,128)S(1)}, u32[]{:S(2)}, u32[]{:S(2)}) %collective-permute-start.20) | collective-permute-done | bytes 131104 | tf_op jit(solution)/shard_map/ppermute | solution.py:331
  104.4 3.8 %collective-permute-done.24.refs_3_ = f32[256,128]{1,0:T(8,128)S(1)} collective-permute-done((f32[256,128]{1,0:T(8,128)S(1)}, f32[256,128]{1,0:T(8,128)S(1)}, u32[]{:S(2)}, u32[]{:S(2)}) %collective-permute-start.24) | collective-permute-done | bytes 131104 | tf_op jit(solution)/shard_map/ppermute | solution.py:331
  108.2 3.9 %collective-permute-done.23.refs_2_ = f32[256,128]{1,0:T(8,128)S(1)} collective-permute-done((f32[256,128]{1,0:T(8,128)S(1)}, f32[256,128]{1,0:T(8,128)S(1)}, u32[]{:S(2)}, u32[]{:S(2)}) %collective-permute-start.23) | collective-permute-done | bytes 131104 | tf_op jit(solution)/shard_map/ppermute | solution.py:331
  119.6 2.6 %assemble.2 = (f32[2048,128]{1,0:T(8,128)}, bf16[2048,128]{1,0:T(8,128)(2,1)}) custom-call(f32[256,128]{1,0:T(8,128)} %copy-done.1, f32[256,128]{1,0:T(8,128)} %copy-done.30, f32[256,128]{1,0:T(8,128)} %copy-done.29, f32[256,128]{1,0:T(8,128)} %copy-done.28, f32[256,128]{1,0:T(8,128)} %copy-done.31, f32[256,128]{1,0:T(8,128)} %copy-done.39, ...), custom_call_target="tpu_custom_call" | custom-call | tf_op jit(solution)/shard_map/assemble/pallas_call | solution.py:314
  122.2 5.6 %time_pass.6 = (f32[256,128]{1,0:T(8,128)}, f32[256,128]{1,0:T(8,128)}, f32[256,128]{1,0:T(8,128)}, f32[256,128]{1,0:T(8,128)}) custom-call(bf16[2048,1024]{1,0:T(8,128)(2,1)} %get-tuple-element.48.refs_0_, bf16[2048,128]{1,0:T(8,128)(2,1)} %get-tuple-element.70.refs_1_, f32[256,128]{1,0:T(8,128)} %copy-done, f32[256,128]{1,0:T(8,128)} %copy-done.6, ...), custom_call_target="tpu_custom_call" | custom-call | tf_op jit(solution)/shard_map/time_pass/pallas_call | solution.py:184
  127.8 3.6 %collective-permute-start.29 = (f32[256,128]{1,0:T(8,128)}, f32[256,128]{1,0:T(8,128)S(1)}, u32[]{:S(2)}, u32[]{:S(2)}) collective-permute-start(f32[256,128]{1,0:T(8,128)} %get-tuple-element.73), channel_id=1, source_target_pairs={{0,8},{8,0},{16,24},{24,16},{1,9},{9,1},{17,25},{25,17},{2,10},{10... | collective-permute-start | bytes 393224 | tf_op jit(solution)/shard_map/ppermute | solution.py:331
  135.5 3.9 %collective-permute-done.30 = f32[256,128]{1,0:T(8,128)S(1)} collective-permute-done((f32[256,128]{1,0:T(8,128)}, f32[256,128]{1,0:T(8,128)S(1)}, u32[]{:S(2)}, u32[]{:S(2)}) %collective-permute-start.30) | collective-permute-done | bytes 131104 | tf_op jit(solution)/shard_map/ppermute | solution.py:331
  144.0 3.6 %collective-permute-done.37.refs_5_ = f32[256,128]{1,0:T(8,128)S(1)} collective-permute-done((f32[256,128]{1,0:T(8,128)S(1)}, f32[256,128]{1,0:T(8,128)S(1)}, u32[]{:S(2)}, u32[]{:S(2)}) %collective-permute-start.37) | collective-permute-done | bytes 131104 | tf_op jit(solution)/shard_map/ppermute | solution.py:331
  149.5 5.7 %time_pass.7 = (f32[256,128]{1,0:T(8,128)}, f32[256,128]{1,0:T(8,128)}, f32[256,128]{1,0:T(8,128)}, f32[256,128]{1,0:T(8,128)}, f32[264,128]{1,0:T(8,128)}, /*in...) custom-call(bf16[2048,1024]{1,0:T(8,128)(2,1)} %get-tuple-element.48.refs_0_, ...), custom_call_target="tpu_custom_call" | custom-call | tf_op jit(solution)/shard_map/time_pass/pallas_call | solution.py:184
  156.6 5.6 %collective-permute-start.41 = (f32[264,128]{1,0:T(8,128)}, f32[264,128]{1,0:T(8,128)S(1)}, u32[]{:S(2)}, u32[]{:S(2)}) collective-permute-start(f32[264,128]{1,0:T(8,128)} %get-tuple-element.84), channel_id=1, source_target_pairs={{0,2},{1,3},{2,4},{3,5},{4,6},{5,7},{9,8},{10,9},{11,10},{12,11},{... | collective-permute-start | bytes 405512 | tf_op jit(solution)/shard_map/ppermute | solution.py:348
  163.5 3.1 %collective-permute-start.38 = (f32[256,128]{1,0:T(8,128)}, f32[256,128]{1,0:T(8,128)S(1)}, u32[]{:S(2)}, u32[]{:S(2)}) collective-permute-start(f32[256,128]{1,0:T(8,128)} %get-tuple-element.81), channel_id=1, source_target_pairs={{0,8},{8,0},{16,24},{24,16},{1,9},{9,1},{17,25},{25,17},{2,10},{10... | collective-permute-start | bytes 393224 | tf_op jit(solution)/shard_map/ppermute | solution.py:331
  178.0 3.8 %collective-permute-done.46.refs_5_ = f32[256,128]{1,0:T(8,128)S(1)} collective-permute-done((f32[256,128]{1,0:T(8,128)S(1)}, f32[256,128]{1,0:T(8,128)S(1)}, u32[]{:S(2)}, u32[]{:S(2)}) %collective-permute-start.46) | collective-permute-done | bytes 131104 | tf_op jit(solution)/shard_map/ppermute | solution.py:331
  183.7 6.7 %load_pass.3 = (f32[1024,128]{1,0:T(8,128)}, f32[256,128]{1,0:T(8,128)}, f32[256,128]{1,0:T(8,128)}, f32[256,128]{1,0:T(8,128)}, f32[256,128]{1,0:T(8,128)}, /*index=5*/f32[1024,128]{1,0:T(8,128)}) custom-call(bf16[2048,1024]{1,0:T(8,128)(2,1)} %get-tuple-element.48.refs_0_, bf16[2048,128]{1,0:T(8,128)(2,1)} %get-tuple-element.70.refs_1_, ...), custom_call_target="tpu_custom_call" | custom-call | tf_op jit(solution)/shard_map/load_pass/pallas_call | solution.py:245
  196.2 2.9 %collective-permute-start.50 = (f32[256,128]{1,0:T(8,128)S(1)}, f32[256,128]{1,0:T(8,128)S(1)}, u32[]{:S(2)}, u32[]{:S(2)}) collective-permute-start(f32[256,128]{1,0:T(8,128)S(1)} %get-tuple-element.95), channel_id=1, source_target_pairs={{0,6},{1,7},{2,4},{3,5},{4,2},{5,3},{6,0},{7,1},{8,14},{9,15},{10,... | collective-permute-start | bytes 393224 | tf_op jit(solution)/shard_map/ppermute | solution.py:331
  200.0 6.3 %collective-permute-done.50 = f32[256,128]{1,0:T(8,128)S(1)} collective-permute-done((f32[256,128]{1,0:T(8,128)S(1)}, f32[256,128]{1,0:T(8,128)S(1)}, u32[]{:S(2)}, u32[]{:S(2)}) %collective-permute-start.50) | collective-permute-done | bytes 131104 | tf_op jit(solution)/shard_map/ppermute | solution.py:331
  206.3 4.1 %collective-permute-done.49 = f32[256,128]{1,0:T(8,128)S(1)} collective-permute-done((f32[256,128]{1,0:T(8,128)S(1)}, f32[256,128]{1,0:T(8,128)S(1)}, u32[]{:S(2)}, u32[]{:S(2)}) %collective-permute-start.49) | collective-permute-done | bytes 131104 | tf_op jit(solution)/shard_map/ppermute | solution.py:331
  215.8 3.8 %collective-permute-done.53.refs_3_ = f32[256,128]{1,0:T(8,128)S(1)} collective-permute-done((f32[256,128]{1,0:T(8,128)S(1)}, f32[256,128]{1,0:T(8,128)S(1)}, u32[]{:S(2)}, u32[]{:S(2)}) %collective-permute-start.53) | collective-permute-done | bytes 131104 | tf_op jit(solution)/shard_map/ppermute | solution.py:331
  219.6 4.0 %collective-permute-done.52.refs_2_ = f32[256,128]{1,0:T(8,128)S(1)} collective-permute-done((f32[256,128]{1,0:T(8,128)S(1)}, f32[256,128]{1,0:T(8,128)S(1)}, u32[]{:S(2)}, u32[]{:S(2)}) %collective-permute-start.52) | collective-permute-done | bytes 131104 | tf_op jit(solution)/shard_map/ppermute | solution.py:331
  226.3 2.6 %assemble.3 = (f32[2048,128]{1,0:T(8,128)}, bf16[2048,128]{1,0:T(8,128)(2,1)}) custom-call(f32[256,128]{1,0:T(8,128)} %copy-done.10, f32[256,128]{1,0:T(8,128)} %copy-done.35, f32[256,128]{1,0:T(8,128)} %copy-done.33, f32[256,128]{1,0:T(8,128)} %copy-done.32, f32[256,128]{1,0:T(8,128)} %copy-done.36, f32[256,128]{1,0:T(8,128)} %copy-done.41, ...), custom_call_target="tpu_custom_call" | custom-call | tf_op jit(solution)/shard_map/assemble/pallas_call | solution.py:314
  (196 shorter events, 90.1 us)
Async XLA Ops:
  8.5 12.1 %collective-permute-start.5 = (f32[104,128]{1,0:T(8,128)}, f32[104,128]{1,0:T(8,128)S(1)}, u32[]{:S(2)}, u32[]{:S(2)}) collective-permute-start(f32[104,128]{1,0:T(8,128)} %get-tuple-element.56), channel_id=1, source_target_pairs={{0,1},{1,2},{2,3},{3,4},{4,5},{5,6},{6,7},{8,9},{9,10},{10,11},{11... | collective-permute-start | bytes 159752 | tf_op jit(solution)/shard_map/ppermute | solution.py:348
  10.9 11.3 %collective-permute-start.3 = (f32[264,128]{1,0:T(8,128)}, f32[264,128]{1,0:T(8,128)S(1)}, u32[]{:S(2)}, u32[]{:S(2)}) collective-permute-start(f32[264,128]{1,0:T(8,128)} %get-tuple-element.54), channel_id=1, source_target_pairs={{0,2},{1,3},{2,4},{3,5},{4,6},{5,7},{9,8},{10,9},{11,10},{12,11},{... | collective-permute-start | bytes 405512 | tf_op jit(solution)/shard_map/ppermute | solution.py:348
  16.7 8.1 %collective-permute-start = (f32[256,128]{1,0:T(8,128)}, f32[256,128]{1,0:T(8,128)S(1)}, u32[]{:S(2)}, u32[]{:S(2)}) collective-permute-start(f32[256,128]{1,0:T(8,128)} %get-tuple-element.51), channel_id=1, source_target_pairs={{0,8},{8,0},{16,24},{24,16},{1,9},{9,1},{17,25},{25,17},{2,10},{10... | collective-permute-start | bytes 393224 | tf_op jit(solution)/shard_map/ppermute | solution.py:331
  20.6 7.8 %collective-permute-start.1 = (f32[256,128]{1,0:T(8,128)}, f32[256,128]{1,0:T(8,128)S(1)}, u32[]{:S(2)}, u32[]{:S(2)}) collective-permute-start(f32[256,128]{1,0:T(8,128)} %get-tuple-element.52), channel_id=1, source_target_pairs={{0,16},{8,24},{16,0},{24,8},{1,17},{9,25},{17,1},{25,9},{2,18},{10... | collective-permute-start | bytes 393224 | tf_op jit(solution)/shard_map/ppermute | solution.py:331
  20.6 7.8 %collective-permute-start.2 = (f32[256,128]{1,0:T(8,128)}, f32[256,128]{1,0:T(8,128)S(1)}, u32[]{:S(2)}, u32[]{:S(2)}) collective-permute-start(f32[256,128]{1,0:T(8,128)} %get-tuple-element.53), channel_id=1, source_target_pairs={{0,24},{8,16},{16,8},{24,0},{1,25},{9,17},{17,9},{25,1},{2,26},{10... | collective-permute-start | bytes 393224 | tf_op jit(solution)/shard_map/ppermute | solution.py:331
  44.1 9.7 %collective-permute-start.14 = (f32[104,128]{1,0:T(8,128)}, f32[104,128]{1,0:T(8,128)S(1)}, u32[]{:S(2)}, u32[]{:S(2)}) collective-permute-start(f32[104,128]{1,0:T(8,128)} %get-tuple-element.64), channel_id=1, source_target_pairs={{0,1},{1,2},{2,3},{3,4},{4,5},{5,6},{6,7},{8,9},{9,10},{10,11},{11... | collective-permute-start | bytes 159752 | tf_op jit(solution)/shard_map/ppermute | solution.py:348
  45.4 9.9 %collective-permute-start.12 = (f32[264,128]{1,0:T(8,128)}, f32[264,128]{1,0:T(8,128)S(1)}, u32[]{:S(2)}, u32[]{:S(2)}) collective-permute-start(f32[264,128]{1,0:T(8,128)} %get-tuple-element.62), channel_id=1, source_target_pairs={{0,2},{1,3},{2,4},{3,5},{4,6},{5,7},{9,8},{10,9},{11,10},{12,11},{... | collective-permute-start | bytes 405512 | tf_op jit(solution)/shard_map/ppermute | solution.py:348
  50.4 7.9 %collective-permute-start.9 = (f32[256,128]{1,0:T(8,128)}, f32[256,128]{1,0:T(8,128)S(1)}, u32[]{:S(2)}, u32[]{:S(2)}) collective-permute-start(f32[256,128]{1,0:T(8,128)} %get-tuple-element.59), channel_id=1, source_target_pairs={{0,8},{8,0},{16,24},{24,16},{1,9},{9,1},{17,25},{25,17},{2,10},{10... | collective-permute-start | bytes 393224 | tf_op jit(solution)/shard_map/ppermute | solution.py:331
  53.7 7.8 %collective-permute-start.10 = (f32[256,128]{1,0:T(8,128)}, f32[256,128]{1,0:T(8,128)S(1)}, u32[]{:S(2)}, u32[]{:S(2)}) collective-permute-start(f32[256,128]{1,0:T(8,128)} %get-tuple-element.60), channel_id=1, source_target_pairs={{0,16},{8,24},{16,0},{24,8},{1,17},{9,25},{17,1},{25,9},{2,18},{10... | collective-permute-start | bytes 393224 | tf_op jit(solution)/shard_map/ppermute | solution.py:331
  53.8 7.8 %collective-permute-start.11 = (f32[256,128]{1,0:T(8,128)}, f32[256,128]{1,0:T(8,128)S(1)}, u32[]{:S(2)}, u32[]{:S(2)}) collective-permute-start(f32[256,128]{1,0:T(8,128)} %get-tuple-element.61), channel_id=1, source_target_pairs={{0,24},{8,16},{16,8},{24,0},{1,25},{9,17},{17,9},{25,1},{2,26},{10... | collective-permute-start | bytes 393224 | tf_op jit(solution)/shard_map/ppermute | solution.py:331
  85.4 8.2 %collective-permute-start.21 = (f32[256,128]{1,0:T(8,128)S(1)}, f32[256,128]{1,0:T(8,128)S(1)}, u32[]{:S(2)}, u32[]{:S(2)}) collective-permute-start(f32[256,128]{1,0:T(8,128)S(1)} %get-tuple-element.98), channel_id=1, source_target_pairs={{0,6},{1,7},{2,4},{3,5},{4,2},{5,3},{6,0},{7,1},{8,14},{9,15},{10,... | collective-permute-start | bytes 393224 | tf_op jit(solution)/shard_map/ppermute | solution.py:331
  85.8 13.1 %collective-permute-start.20 = (f32[256,128]{1,0:T(8,128)S(1)}, f32[256,128]{1,0:T(8,128)S(1)}, u32[]{:S(2)}, u32[]{:S(2)}) collective-permute-start(f32[256,128]{1,0:T(8,128)S(1)} %get-tuple-element.99), channel_id=1, source_target_pairs={{0,4},{1,5},{2,6},{3,7},{4,0},{5,1},{6,2},{7,3},{8,12},{9,13},{10,... | collective-permute-start | bytes 393224 | tf_op jit(solution)/shard_map/ppermute | solution.py:331
  99.9 8.3 %collective-permute-start.24 = (f32[256,128]{1,0:T(8,128)S(1)}, f32[256,128]{1,0:T(8,128)S(1)}, u32[]{:S(2)}, u32[]{:S(2)}) collective-permute-start(f32[256,128]{1,0:T(8,128)S(1)} %fusion.11.refs_0_), channel_id=1, source_target_pairs={{0,6},{1,7},{2,4},{3,5},{4,2},{5,3},{6,0},{7,1},{8,14},{9,15},{10,... | collective-permute-start | bytes 393224 | tf_op jit(solution)/shard_map/ppermute | solution.py:331
  101.8 10.3 %collective-permute-start.23 = (f32[256,128]{1,0:T(8,128)S(1)}, f32[256,128]{1,0:T(8,128)S(1)}, u32[]{:S(2)}, u32[]{:S(2)}) collective-permute-start(f32[256,128]{1,0:T(8,128)S(1)} %fusion.11.refs_0_), channel_id=1, source_target_pairs={{0,4},{1,5},{2,6},{3,7},{4,0},{5,1},{6,2},{7,3},{8,12},{9,13},{10,... | collective-permute-start | bytes 393224 | tf_op jit(solution)/shard_map/ppermute | solution.py:331
  101.8 10.3 %collective-permute-start.22 = (f32[256,128]{1,0:T(8,128)S(1)}, f32[256,128]{1,0:T(8,128)S(1)}, u32[]{:S(2)}, u32[]{:S(2)}) collective-permute-start(f32[256,128]{1,0:T(8,128)S(1)} %fusion.11.refs_0_), channel_id=1, source_target_pairs={{0,2},{1,3},{2,0},{3,1},{4,6},{5,7},{6,4},{7,5},{8,10},{9,11},{10,... | collective-permute-start | bytes 393224 | tf_op jit(solution)/shard_map/ppermute | solution.py:331
  104.3 10.2 %collective-permute-start.25 = (f32[256,128]{1,0:T(8,128)S(1)}, f32[256,128]{1,0:T(8,128)S(1)}, u32[]{:S(2)}, u32[]{:S(2)}) collective-permute-start(f32[256,128]{1,0:T(8,128)S(1)} %fusion.11.refs_0_), channel_id=1, source_target_pairs={{0,1},{1,0},{2,3},{3,2},{4,5},{5,4},{6,7},{7,6},{8,9},{9,8},{10,11... | collective-permute-start | bytes 393224 | tf_op jit(solution)/shard_map/ppermute | solution.py:331
  108.2 8.6 %collective-permute-start.28 = (f32[256,128]{1,0:T(8,128)S(1)}, f32[256,128]{1,0:T(8,128)S(1)}, u32[]{:S(2)}, u32[]{:S(2)}) collective-permute-start(f32[256,128]{1,0:T(8,128)S(1)} %collective-permute-done.24.refs_3_), channel_id=1, source_target_pairs={{0,1},{1,0},{2,3},{3,2},{4,5},{5,4},{6,7},{7,6},{8,9},{9,8},{10,11... | collective-permute-start | bytes 393224 | tf_op jit(solution)/shard_map/ppermute | solution.py:331
  112.6 18.8 %collective-permute-start.34 = (f32[104,128]{1,0:T(8,128)}, f32[104,128]{1,0:T(8,128)S(1)}, u32[]{:S(2)}, u32[]{:S(2)}) collective-permute-start(f32[104,128]{1,0:T(8,128)} %get-tuple-element.78), channel_id=1, source_target_pairs={{0,1},{1,2},{2,3},{3,4},{4,5},{5,6},{6,7},{8,9},{9,10},{10,11},{11... | collective-permute-start | bytes 159752 | tf_op jit(solution)/shard_map/ppermute | solution.py:348
  114.6 18.3 %collective-permute-start.32 = (f32[264,128]{1,0:T(8,128)}, f32[264,128]{1,0:T(8,128)S(1)}, u32[]{:S(2)}, u32[]{:S(2)}) collective-permute-start(f32[264,128]{1,0:T(8,128)} %get-tuple-element.76), channel_id=1, source_target_pairs={{0,2},{1,3},{2,4},{3,5},{4,6},{5,7},{9,8},{10,9},{11,10},{12,11},{... | collective-permute-start | bytes 405512 | tf_op jit(solution)/shard_map/ppermute | solution.py:348
  116.8 16.2 %collective-permute-start.33 = (f32[264,128]{1,0:T(8,128)}, f32[264,128]{1,0:T(8,128)S(1)}, u32[]{:S(2)}, u32[]{:S(2)}) collective-permute-start(f32[264,128]{1,0:T(8,128)} %get-tuple-element.77), channel_id=1, source_target_pairs={{1,0},{2,1},{3,2},{4,3},{5,4},{6,5},{7,6},{8,10},{9,11},{10,12},{1... | collective-permute-start | bytes 405512 | tf_op jit(solution)/shard_map/ppermute | solution.py:348
  127.8 7.7 %collective-permute-start.29 = (f32[256,128]{1,0:T(8,128)}, f32[256,128]{1,0:T(8,128)S(1)}, u32[]{:S(2)}, u32[]{:S(2)}) collective-permute-start(f32[256,128]{1,0:T(8,128)} %get-tuple-element.73), channel_id=1, source_target_pairs={{0,8},{8,0},{16,24},{24,16},{1,9},{9,1},{17,25},{25,17},{2,10},{10... | collective-permute-start | bytes 393224 | tf_op jit(solution)/shard_map/ppermute | solution.py:331
  131.4 8.0 %collective-permute-start.30 = (f32[256,128]{1,0:T(8,128)}, f32[256,128]{1,0:T(8,128)S(1)}, u32[]{:S(2)}, u32[]{:S(2)}) collective-permute-start(f32[256,128]{1,0:T(8,128)} %get-tuple-element.74), channel_id=1, source_target_pairs={{0,16},{8,24},{16,0},{24,8},{1,17},{9,25},{17,1},{25,9},{2,18},{10... | collective-permute-start | bytes 393224 | tf_op jit(solution)/shard_map/ppermute | solution.py:331
  131.4 8.0 %collective-permute-start.31 = (f32[256,128]{1,0:T(8,128)}, f32[256,128]{1,0:T(8,128)S(1)}, u32[]{:S(2)}, u32[]{:S(2)}) collective-permute-start(f32[256,128]{1,0:T(8,128)} %get-tuple-element.75), channel_id=1, source_target_pairs={{0,24},{8,16},{16,8},{24,0},{1,25},{9,17},{17,9},{25,1},{2,26},{10... | collective-permute-start | bytes 393224 | tf_op jit(solution)/shard_map/ppermute | solution.py:331
  155.2 11.4 %collective-permute-start.43 = (f32[104,128]{1,0:T(8,128)}, f32[104,128]{1,0:T(8,128)S(1)}, u32[]{:S(2)}, u32[]{:S(2)}) collective-permute-start(f32[104,128]{1,0:T(8,128)} %get-tuple-element.86), channel_id=1, source_target_pairs={{0,1},{1,2},{2,3},{3,4},{4,5},{5,6},{6,7},{8,9},{9,10},{10,11},{11... | collective-permute-start | bytes 159752 | tf_op jit(solution)/shard_map/ppermute | solution.py:348
  156.6 11.5 %collective-permute-start.41 = (f32[264,128]{1,0:T(8,128)}, f32[264,128]{1,0:T(8,128)S(1)}, u32[]{:S(2)}, u32[]{:S(2)}) collective-permute-start(f32[264,128]{1,0:T(8,128)} %get-tuple-element.84), channel_id=1, source_target_pairs={{0,2},{1,3},{2,4},{3,5},{4,6},{5,7},{9,8},{10,9},{11,10},{12,11},{... | collective-permute-start | bytes 405512 | tf_op jit(solution)/shard_map/ppermute | solution.py:348
  163.5 7.6 %collective-permute-start.38 = (f32[256,128]{1,0:T(8,128)}, f32[256,128]{1,0:T(8,128)S(1)}, u32[]{:S(2)}, u32[]{:S(2)}) collective-permute-start(f32[256,128]{1,0:T(8,128)} %get-tuple-element.81), channel_id=1, source_target_pairs={{0,8},{8,0},{16,24},{24,16},{1,9},{9,1},{17,25},{25,17},{2,10},{10... | collective-permute-start | bytes 393224 | tf_op jit(solution)/shard_map/ppermute | solution.py:331
  196.2 10.1 %collective-permute-start.50 = (f32[256,128]{1,0:T(8,128)S(1)}, f32[256,128]{1,0:T(8,128)S(1)}, u32[]{:S(2)}, u32[]{:S(2)}) collective-permute-start(f32[256,128]{1,0:T(8,128)S(1)} %get-tuple-element.95), channel_id=1, source_target_pairs={{0,6},{1,7},{2,4},{3,5},{4,2},{5,3},{6,0},{7,1},{8,14},{9,15},{10,... | collective-permute-start | bytes 393224 | tf_op jit(solution)/shard_map/ppermute | solution.py:331
  199.1 11.3 %collective-permute-start.49 = (f32[256,128]{1,0:T(8,128)S(1)}, f32[256,128]{1,0:T(8,128)S(1)}, u32[]{:S(2)}, u32[]{:S(2)}) collective-permute-start(f32[256,128]{1,0:T(8,128)S(1)} %get-tuple-element.96), channel_id=1, source_target_pairs={{0,4},{1,5},{2,6},{3,7},{4,0},{5,1},{6,2},{7,3},{8,12},{9,13},{10,... | collective-permute-start | bytes 393224 | tf_op jit(solution)/shard_map/ppermute | solution.py:331
  211.3 8.3 %collective-permute-start.53 = (f32[256,128]{1,0:T(8,128)S(1)}, f32[256,128]{1,0:T(8,128)S(1)}, u32[]{:S(2)}, u32[]{:S(2)}) collective-permute-start(f32[256,128]{1,0:T(8,128)S(1)} %fusion.5.refs_0_), channel_id=1, source_target_pairs={{0,6},{1,7},{2,4},{3,5},{4,2},{5,3},{6,0},{7,1},{8,14},{9,15},{10,... | collective-permute-start | bytes 393224 | tf_op jit(solution)/shard_map/ppermute | solution.py:331
  213.6 10.0 %collective-permute-start.52 = (f32[256,128]{1,0:T(8,128)S(1)}, f32[256,128]{1,0:T(8,128)S(1)}, u32[]{:S(2)}, u32[]{:S(2)}) collective-permute-start(f32[256,128]{1,0:T(8,128)S(1)} %fusion.5.refs_0_), channel_id=1, source_target_pairs={{0,4},{1,5},{2,6},{3,7},{4,0},{5,1},{6,2},{7,3},{8,12},{9,13},{10,... | collective-permute-start | bytes 393224 | tf_op jit(solution)/shard_map/ppermute | solution.py:331
  213.6 10.0 %collective-permute-start.51 = (f32[256,128]{1,0:T(8,128)S(1)}, f32[256,128]{1,0:T(8,128)S(1)}, u32[]{:S(2)}, u32[]{:S(2)}) collective-permute-start(f32[256,128]{1,0:T(8,128)S(1)} %fusion.5.refs_0_), channel_id=1, source_target_pairs={{0,2},{1,3},{2,0},{3,1},{4,6},{5,7},{6,4},{7,5},{8,10},{9,11},{10,... | collective-permute-start | bytes 393224 | tf_op jit(solution)/shard_map/ppermute | solution.py:331
  215.8 8.3 %collective-permute-start.54 = (f32[256,128]{1,0:T(8,128)S(1)}, f32[256,128]{1,0:T(8,128)S(1)}, u32[]{:S(2)}, u32[]{:S(2)}) collective-permute-start(f32[256,128]{1,0:T(8,128)S(1)} %fusion.5.refs_0_), channel_id=1, source_target_pairs={{0,1},{1,0},{2,3},{3,2},{4,5},{5,4},{6,7},{7,6},{8,9},{9,8},{10,11... | collective-permute-start | bytes 393224 | tf_op jit(solution)/shard_map/ppermute | solution.py:331
  (72 other events, 385.7 us)

commit v2 on v1

v2 whole, which is shorter than its diff:
```python
import jax
import jax.numpy as jnp
from jax import lax
from jax.experimental import pallas as pl
from jax.experimental.pallas import tpu as pltpu
from jax.sharding import PartitionSpec as P

LAG = 1440
OUTER = 2
TIME_STEPS = 2

smooth = 4.0
shrink = 0.1
margin = 32.0
hidden = 64.0
PAD = 8
F32 = jnp.float32
BF16 = jnp.bfloat16
VMEM = pl.BlockSpec(memory_space=pltpu.VMEM)
HBM = pl.BlockSpec(memory_space=pltpu.HBM)


def dot_nt(a, b):
    return lax.dot_general(a, b, (((1,), (1,)), ((), ())), preferred_element_type=F32)


def dot_tn(a, b):
    return lax.dot_general(a, b, (((0,), (0,)), ((), ())), preferred_element_type=F32)


def dot_nn(a, b):
    return lax.dot_general(a, b, (((1,), (0,)), ((), ())), preferred_element_type=F32)


def grant(mib):
    return pltpu.CompilerParams(vmem_limit_bytes=mib * 2**20)


def up8(value):
    return -(-value // 8) * 8


class Plan:
    def __init__(self, n_s, n_t, series, minutes, rank):
        self.n_s, self.n_t, self.series, self.minutes, self.rank = n_s, n_t, series, minutes, rank
        self.rows = minutes // n_s
        self.n_z = n_t // 2
        self.block = series // n_t
        self.half = series // 2
        self.need = []
        for s in range(n_s):
            first = s * self.rows
            spans = [("back", first - LAG, self.rows + 1), ("far", first + LAG - 1, self.rows + 1)]
            if s == 0:
                spans.append(("prev", -1, 1))
            if s == n_s - 1:
                spans.append(("next", minutes, 1))
            by_delta, filled = {}, {}
            for kind, row, count in spans:
                at = 0
                while at < count:
                    delta = (row + at) // minutes
                    local = (row + at) % minutes
                    size = min(count - at, minutes - local)
                    assert delta != 0
                    offset = filled.get(delta, 0)
                    by_delta.setdefault(delta, []).append((kind, at, local, size, offset))
                    filled[delta] = offset + up8(size)
                    at += size
            self.need.append((by_delta, filled))
        reach = max(abs(delta) for by_delta, filled in self.need for delta in by_delta)
        self.exchanges = [(step, parity) for step in range(1, reach + 1) for parity in (0, 1)]
        self.length, self.pairs = [], []
        for step, parity in self.exchanges:
            sizes = [filled.get(delta, 0) for by_delta, filled in self.need for delta in (step, -step)]
            self.length.append(max(sizes + [8]))
            self.pairs.append([(t, t + self.delta(e, t)) for e in [(step, parity)] for t in range(n_t)
                               if 0 <= t + self.delta(e, t) < n_t])

    def delta(self, exchange, t):
        step, parity = exchange
        return step if (t // step) % 2 == parity else -step

    def each_part(self, sending, act):
        s = lax.axis_index("series")
        t = lax.axis_index("tm")
        for value in range(self.n_s):
            for step in sorted({step for step, parity in self.exchanges}):
                for low in (0, 1):
                    slots = [(slot, e) for slot, e in enumerate(self.exchanges) if e[0] == step]

                    @pl.when(jnp.logical_and(s == value, (t // step) % 2 == low))
                    def _():
                        for slot, exchange in slots:
                            delta = self.delta(exchange, low * step)
                            for part in self.need[value][0].get(-delta if sending else delta, []):
                                act(slot, part)


def load_x(plan, x_refs, xs):
    s = lax.axis_index("series")
    rows = plan.rows
    if len(x_refs) == 1:
        xs[pl.ds(PAD, plan.minutes), :] = x_refs[0][...]
    else:
        for k in range(plan.n_s):
            start = pl.multiple_of(PAD + jnp.bitwise_xor(s, k) * rows, 8)
            xs[pl.ds(start, rows), :] = x_refs[k][...]


def pack_halo(plan, xs, h_refs, win):
    s = lax.axis_index("series")
    start = pl.multiple_of(s * plan.rows, 8)
    win[...] = xs[pl.ds(start, plan.rows + 2 * PAD), :]

    def act(slot, part):
        kind, at, local, size, offset = part
        h_refs[slot][pl.ds(offset, size), :] = xs[pl.ds(PAD + local, size), :]

    plan.each_part(True, act)


def residual(prod, obs):
    obs = obs.astype(F32)
    return jnp.where(obs < 0.5 * hidden, prod - obs, 0.0).astype(BF16)


def halo_shapes(plan):
    shapes = [jax.ShapeDtypeStruct((length, plan.rank), F32) for length in plan.length]
    return shapes + [jax.ShapeDtypeStruct((plan.rows + 2 * PAD, plan.rank), F32)]


def block_start(plan, c):
    t = lax.axis_index("tm")
    core, z = t % 2, t // 2
    side = core if c < plan.n_z else 1 - core
    return pl.multiple_of(side * plan.half + jnp.bitwise_xor(z, c % plan.n_z) * plan.block, plan.block)


def time_pass(plan, data, loads, xp, halo):
    first = len(data) == 2
    n_s, rows, series, minutes, rank = plan.n_s, plan.rows, plan.series, plan.minutes, plan.rank
    chunk = series // 4
    count = series // chunk
    n_x, n_f = len(xp), len(loads)
    n_h = len(plan.exchanges) + 1 if halo else 0

    def kernel(*refs):
        refs = list(refs)
        d_refs = [refs.pop(0) for _ in data]
        f_refs = [refs.pop(0) for _ in loads]
        x_refs = [refs.pop(0) for _ in range(n_x)]
        g_refs = [refs.pop(0) for _ in range(n_s)]
        h_refs = [refs.pop(0) for _ in range(n_h)]
        f = f_refs[0]
        if n_f > 1:
            f = refs.pop(0)
        held = refs.pop(0) if first else d_refs[0]
        xs, acc = refs[:2]
        if first:
            seen, sem = refs[2:]
            copies = []
            for c in range(count):
                span = pl.ds(c * chunk, chunk)
                copies.append([pltpu.make_async_copy(src.at[span, :], dst.at[span, :], sem.at[i, c])
                               for i, (src, dst) in enumerate(zip(d_refs, (held, seen)))])
            for group in copies:
                for copy in group:
                    copy.start()
        load_x(plan, x_refs, xs)
        if n_f > 1:
            for c in range(n_f):
                f[pl.ds(block_start(plan, c), plan.block), :] = f_refs[c][...].astype(BF16)
        if halo:
            pack_halo(plan, xs, h_refs[:-1], h_refs[-1])
        xb = xs[pl.ds(PAD, minutes), :].astype(BF16)
        for c in range(count):
            span = pl.ds(c * chunk, chunk)
            if first:
                for copy in copies[c]:
                    copy.wait()
                held[span, :] = jnp.where(seen[span, :] > 0, held[span, :], jnp.full((), hidden, BF16))
            fb = f[span, :].astype(BF16)
            part = dot_tn(fb, residual(dot_nt(fb, xb), held[span, :]))
            if c == 0:
                acc[...] = part
            else:
                acc[...] += part
        s = lax.axis_index("series")
        for k in range(n_s):
            start = pl.multiple_of(jnp.bitwise_xor(s, k) * rows, 128)
            g_refs[k][...] = acc[:, pl.ds(start, rows)].T

    out_shape = [jax.ShapeDtypeStruct((rows, rank), F32) for _ in range(n_s)]
    if halo:
        out_shape += halo_shapes(plan)
    if n_f > 1:
        out_shape.append(jax.ShapeDtypeStruct((series, rank), BF16))
    if first:
        out_shape.append(jax.ShapeDtypeStruct((series, minutes), BF16))
    scratch = [pltpu.VMEM((minutes + 2 * PAD, rank), F32), pltpu.VMEM((rank, minutes), F32)]
    if first:
        scratch += [pltpu.VMEM((series, minutes), BF16), pltpu.SemaphoreType.DMA((2, count))]
    outs = list(pl.pallas_call(
        kernel,
        in_specs=[HBM if first else VMEM] * len(data) + [VMEM] * (n_f + n_x),
        out_specs=[VMEM] * len(out_shape),
        out_shape=out_shape,
        scratch_shapes=scratch,
        compiler_params=grant(54 if first else 16),
        name="time_pass",
    )(*data, *loads, *xp))
    grads = outs[:n_s]
    halos = outs[n_s:n_s + n_h]
    return grads, halos, outs[n_s + n_h:]


def load_pass(plan, data, f, xp, other, halo, whole):
    series, minutes, rank = plan.series, plan.minutes, plan.rank
    block, n_z = plan.block, plan.n_z
    n_x = len(xp)
    n_h = len(plan.exchanges) + 1 if halo else 0

    def kernel(*refs):
        refs = list(refs)
        d, f_ref = refs.pop(0), refs.pop(0)
        x_refs = [refs.pop(0) for _ in range(n_x)]
        g_refs = [refs.pop(0) for _ in range(1 if other else n_z)]
        h_refs = [refs.pop(0) for _ in range(n_h)]
        x_out = refs.pop(0) if whole else None
        xs = refs[0]
        load_x(plan, x_refs, xs)
        xb = xs[pl.ds(PAD, minutes), :].astype(BF16)
        for c in range(n_z):
            span = pl.ds(block_start(plan, c + n_z if other else c), block)
            rb = residual(dot_nt(f_ref[span, :].astype(BF16), xb), d[span, :])
            part = dot_nn(rb, xb)
            if other:
                g_refs[0][pl.ds(c * block, block), :] = part
            else:
                g_refs[c][...] = part
        if halo:
            pack_halo(plan, xs, h_refs[:-1], h_refs[-1])
        if whole:
            x_out[...] = xs[pl.ds(PAD, minutes), :]

    if other:
        out_shape = [jax.ShapeDtypeStruct((plan.half, rank), F32)]
    else:
        out_shape = [jax.ShapeDtypeStruct((block, rank), F32) for _ in range(n_z)]
    n_g = len(out_shape)
    if halo:
        out_shape += halo_shapes(plan)
    if whole:
        out_shape.append(jax.ShapeDtypeStruct((minutes, rank), F32))
    outs = list(pl.pallas_call(
        kernel,
        in_specs=[VMEM] * (2 + n_x),
        out_specs=[VMEM] * len(out_shape),
        out_shape=out_shape,
        scratch_shapes=[pltpu.VMEM((minutes + 2 * PAD, rank), F32)],
        compiler_params=grant(16),
        name="load_other" if other else "load_mine",
    )(data, f, *xp))
    return outs[:n_g], outs[n_g:n_g + n_h], outs[n_g + n_h:]


def smoothing(plan, win, halos, lag_weights):
    rows, rank = plan.rows, plan.rank
    total = plan.minutes * plan.n_t

    def kernel(*refs):
        refs = list(refs)
        win_ref = refs.pop(0)
        h_refs = [refs.pop(0) for _ in plan.exchanges]
        w_ref, out, xw, far, near = refs
        s = lax.axis_index("series")
        t = lax.axis_index("tm")
        xw[...] = win_ref[...]

        def act(slot, part):
            kind, at, local, size, offset = part
            target, place = {"back": (near, at), "far": (far, at),
                             "prev": (xw, PAD - 1), "next": (xw, PAD + rows)}[kind]
            target[pl.ds(place, size), :] = h_refs[slot][pl.ds(offset, size), :]

        plan.each_part(False, act)
        w0 = w_ref[0:1, :]
        w1 = w_ref[1:2, :]
        x = xw[pl.ds(PAD, rows), :]
        here = t * plan.minutes + s * rows + lax.broadcasted_iota(jnp.int32, (rows, rank), 0)
        resid = x - w0 * xw[pl.ds(PAD - 1, rows), :] - w1 * near[pl.ds(0, rows), :]
        after_one = xw[pl.ds(PAD + 1, rows), :] - w0 * x - w1 * near[pl.ds(1, rows), :]
        after_far = far[pl.ds(1, rows), :] - w0 * far[pl.ds(0, rows), :] - w1 * x
        after_one = jnp.where(here + 1 < total, after_one, 0.0)
        after_far = jnp.where(here + LAG < total, after_far, 0.0)
        out[...] = smooth * (resid - w0 * after_one - w1 * after_far)

    return pl.pallas_call(
        kernel,
        in_specs=[VMEM] * (2 + len(plan.exchanges)),
        out_specs=VMEM,
        out_shape=jax.ShapeDtypeStruct((rows, rank), F32),
        scratch_shapes=[pltpu.VMEM((rows + 2 * PAD, rank), F32), pltpu.VMEM((up8(rows + 1), rank), F32),
                        pltpu.VMEM((up8(rows + 1), rank), F32)],
        compiler_params=grant(8),
        name="smoothing",
    )(win, *halos, lag_weights)


def assemble(plan, blocks):
    def kernel(*refs):
        for c, ref in enumerate(refs[:-1]):
            refs[-1][pl.ds(block_start(plan, c), plan.block), :] = ref[...]

    return pl.pallas_call(
        kernel,
        in_specs=[VMEM] * len(blocks),
        out_specs=VMEM,
        out_shape=jax.ShapeDtypeStruct((plan.series, plan.rank), F32),
        compiler_params=grant(8),
        name="assemble",
    )(*blocks)


def body(observed, mask, loadings, factors, lag_weights):
    n_s, n_t = lax.axis_size("series"), lax.axis_size("tm")
    plan = Plan(n_s, n_t, loadings.shape[0], factors.shape[0], loadings.shape[1])
    step_time = 1.0 / (plan.series * n_s / plan.rank + margin)
    step_load = 1.0 / (plan.minutes * n_t)
    rows, n_z, block = plan.rows, plan.n_z, plan.block

    def swap(value, axis, count, k):
        return lax.ppermute(value, axis, [(i, i ^ k) for i in range(count)])

    t = lax.axis_index("tm")
    own_start = (t % 2) * plan.half + (t // 2) * block
    own_loads = lax.dynamic_slice_in_dim(loadings, own_start, block, 0)
    loads = [loadings]
    data = [observed, mask]
    xp = [factors]
    halos = []
    for outer in range(OUTER):
        last = outer + 1 == OUTER
        for inner in range(TIME_STEPS):
            grads, made, extra = time_pass(plan, data, loads, xp, not halos)
            if len(data) > 1:
                data = [extra.pop()]
            if len(loads) > 1:
                loads = [extra.pop()]
            halos = halos or made
            got = [swap(grads[k], "series", n_s, k) for k in range(1, n_s)]
            sent = [lax.ppermute(h, "tm", pairs) for h, pairs in zip(halos[:-1], plan.pairs)]
            win = halos[-1]
            smooth_grad = smoothing(plan, win, sent, lag_weights)
            share = grads[0]
            for value in got:
                share = share + value
            own = win[PAD:PAD + rows] - step_time * (share + smooth_grad)
            xp = [own] + [swap(own, "series", n_s, k) for k in range(1, n_s)]
            halos = []
        (other,), _, _ = load_pass(plan, data[0], loads[0], xp, True, False, False)
        crossed = swap(other, "tm", n_t, 1)
        mine, halos, whole = load_pass(plan, data[0], loads[0], xp, False, not last, last)
        mine = [m + crossed[k * block:(k + 1) * block] for k, m in enumerate(mine)]
        total = mine[0]
        for k in range(1, n_z):
            total = total + swap(mine[k], "tm", n_t, 2 * k)
        own_loads = own_loads - step_load * (total + shrink * own_loads)
        near = [own_loads] + [swap(own_loads, "tm", n_t, 2 * k) for k in range(1, n_z)]
        loads = near + [swap(value, "tm", n_t, 1) for value in near]
    return (assemble(plan, loads), whole[0])


def solution(mesh):
    in_specs = (P("series", "tm"), P("series", "tm"), P("series", None), P("tm", None), P())
    out_specs = (P("series", None), P("tm", None))
    return jax.shard_map(body, mesh=mesh, in_specs=in_specs, out_specs=out_specs, check_vma=False)
```

time: 230 us -> 188 us (0.82)
  Pallas kernels: 51.5 us -> 26.1 us
  starting transfers between devices: 82.4 us -> 67.9 us
  waiting for transfers between devices: 76 us -> 84.5 us
  other arithmetic: 8.44 us -> 2.94 us
  local copies, waits for them, and re-layouts: 9.29 us -> 5.28 us
    pallas_call x12 -> x13, Pallas kernels: 51.5 us -> 26.1 us  [the longest x4 17.4 us: time_pass(): pl.pallas_call(kernel, in_specs=[HBM if first else VMEM] * len(data) + [V...]
    ppermute x12 -> x16, starting transfers between devices: 28.4 us -> 18.9 us  [body(): lax.ppermute(h, 'tm', pairs)]
    ppermute x46, starting transfers between devices: 54 us -> 48.9 us  [swap(): return lax.ppermute(value, axis, [(i, i ^ k) for i in range(count)])]
    ppermute x12 -> x16, waiting for transfers between devices: 0.03 us -> 4.87 us  [body(): lax.ppermute(h, 'tm', pairs)]
    unnamed x92 -> x10, local copies, waits for them, and re-layouts: 9.29 us -> 5.28 us
    ppermute x46, waiting for transfers between devices: 76 us -> 79.7 us  [swap(): return lax.ppermute(value, axis, [(i, i ^ k) for i in range(count)])]
    sub x4, other arithmetic: 4.29 us -> 1.17 us  [body(): own = win[PAD:PAD + rows] - step_time * (share + smooth_grad)]
  transfers between devices with their start and end apart: 58 -> 62, of which waited for: 30 -> 33; matrix products, arithmetic and copies ran while one was open for 0% -> 0% of each run, Pallas kernels for 7% -> 4%
where the time goes in v2:
time: 188 us
  waiting for transfers between devices  84.5 us (45%)
  starting transfers between devices  67.9 us (36%)
  Pallas kernels  26.1 us (14%)
  local copies, waits for them, and re-layouts  5.28 us (3%)
  other arithmetic  2.94 us (2%)
    ppermute x46, waiting for transfers between devices, swap(): return lax.ppermute(value, axis, [(i, i ^ k) for i in range(count)])  79.7 us
    ppermute x46, starting transfers between devices, swap(): return lax.ppermute(value, axis, [(i, i ^ k) for i in range(count)])  48.9 us
    ppermute x16, starting transfers between devices, body(): lax.ppermute(h, 'tm', pairs)  18.9 us
    pallas_call x4, Pallas kernels, time_pass(): pl.pallas_call(kernel, in_specs=[HBM if first else VMEM] * len(data) + [V...  17.4 us
    pallas_call x4, Pallas kernels, load_pass(): pl.pallas_call(kernel, in_specs=[VMEM] * (2 + n_x), out_specs=[VMEM] * le...  6.58 us
    unnamed x10, local copies, waits for them, and re-layouts  5.28 us
    ppermute x16, waiting for transfers between devices, body(): lax.ppermute(h, 'tm', pairs)  4.87 us
  transfers between devices with their start and end apart: 62, of which 33 were waited for; matrix products, arithmetic and copies ran while one was open for 0% of the time, Pallas kernels for 4%

profile of v2, /device:TPU:0, one launch (start us, length us, event | category | flops | bytes accessed | tf_op | source)
XLA Modules:
  0.0 187.6 jit_solution(15177349653534467873)
XLA Ops:
  0.7 8.5 %time_pass.4 = (f32[256,128]{1,0:T(8,128)}, f32[256,128]{1,0:T(8,128)}, f32[256,128]{1,0:T(8,128)}, f32[256,128]{1,0:T(8,128)}, f32[264,128]{1,0:T(8,128)}, /*in...) custom-call(bf16[2048,1024]{1,0:T(8,128)(2,1)} %refs_0_.1, ...), custom_call_target="tpu_custom_call" | custom-call | tf_op jit(solution)/shard_map/time_pass/pallas_call | solution.py:204
  10.4 3.9 %collective-permute-start.5 = (f32[264,128]{1,0:T(8,128)}, f32[264,128]{1,0:T(8,128)S(1)}, u32[]{:S(2)}, u32[]{:S(2)}) collective-permute-start(f32[264,128]{1,0:T(8,128)} %get-tuple-element.57), channel_id=1, source_target_pairs={{0,2},{1,3},{2,0},{3,1},{4,6},{5,7},{6,4},{7,5},{8,10},{9,11},{10,... | collective-permute-start | bytes 405512 | tf_op jit(solution)/shard_map/ppermute | solution.py:353
  21.4 4.6 %collective-permute-done.1 = f32[256,128]{1,0:T(8,128)S(1)} collective-permute-done((f32[256,128]{1,0:T(8,128)}, f32[256,128]{1,0:T(8,128)S(1)}, u32[]{:S(2)}, u32[]{:S(2)}) %collective-permute-start.1) | collective-permute-done | bytes 131104 | tf_op jit(solution)/shard_map/ppermute | solution.py:334
  30.6 3.8 %collective-permute-done.9.refs_5_ = f32[256,128]{1,0:T(8,128)S(1)} collective-permute-done((f32[256,128]{1,0:T(8,128)S(1)}, f32[256,128]{1,0:T(8,128)S(1)}, u32[]{:S(2)}, u32[]{:S(2)}) %collective-permute-start.9) | collective-permute-done | bytes 131104 | tf_op jit(solution)/shard_map/ppermute | solution.py:334
  36.0 2.2 %copy-done = bf16[2048,1024]{1,0:T(8,128)(2,1)S(1)} copy-done((bf16[2048,1024]{1,0:T(8,128)(2,1)S(1)}, bf16[2048,1024]{1,0:T(8,128)(2,1)}, u32[]{:S(2)}) %copy-start) | copy-done | bytes 4194328
  38.2 3.0 %time_pass.5 = (f32[256,128]{1,0:T(8,128)S(1)}, f32[256,128]{1,0:T(8,128)S(1)}, f32[256,128]{1,0:T(8,128)S(1)}, f32[256,128]{1,0:T(8,128)S(1)}, f32[264,128]{1,0...) custom-call(bf16[2048,1024]{1,0:T(8,128)(2,1)S(1)} %copy-done, ...), custom_call_target="tpu_custom_call" | custom-call | tf_op jit(solution)/shard_map/time_pass/pallas_call | solution.py:204
  41.9 3.4 %collective-permute-start.15 = (f32[264,128]{1,0:T(8,128)S(1)}, f32[264,128]{1,0:T(8,128)S(1)}, u32[]{:S(2)}, u32[]{:S(2)}) collective-permute-start(f32[264,128]{1,0:T(8,128)S(1)} %get-tuple-element.66), channel_id=1, source_target_pairs={{0,2},{1,3},{2,0},{3,1},{4,6},{5,7},{6,4},{7,5},{8,10},{9,11},{10,... | collective-permute-start | bytes 405512 | tf_op jit(solution)/shard_map/ppermute | solution.py:353
  51.8 3.8 %collective-permute-done.11 = f32[256,128]{1,0:T(8,128)S(1)} collective-permute-done((f32[256,128]{1,0:T(8,128)S(1)}, f32[256,128]{1,0:T(8,128)S(1)}, u32[]{:S(2)}, u32[]{:S(2)}) %collective-permute-start.11) | collective-permute-done | bytes 131104 | tf_op jit(solution)/shard_map/ppermute | solution.py:334
  59.2 3.7 %collective-permute-done.19.refs_5_.refs_12_ = f32[256,128]{1,0:T(8,128)S(1)} collective-permute-done((f32[256,128]{1,0:T(8,128)S(1)}, f32[256,128]{1,0:T(8,128)S(1)}, u32[]{:S(2)}, u32[]{:S(2)}) %collective-permute-start.19) | collective-permute-done | bytes 131104 | tf_op jit(solution)/shard_map/ppermute | solution.py:334
  70.2 3.2 %collective-permute-start.23 = (f32[256,128]{1,0:T(8,128)S(1)}, f32[256,128]{1,0:T(8,128)S(1)}, u32[]{:S(2)}, u32[]{:S(2)}) collective-permute-start(f32[256,128]{1,0:T(8,128)S(1)} %get-tuple-element.100), channel_id=1, source_target_pairs={{0,6},{1,7},{2,4},{3,5},{4,2},{5,3},{6,0},{7,1},{8,14},{9,15},{10,... | collective-permute-start | bytes 393224 | tf_op jit(solution)/shard_map/ppermute | solution.py:334
  74.6 6.2 %collective-permute-done.23 = f32[256,128]{1,0:T(8,128)S(1)} collective-permute-done((f32[256,128]{1,0:T(8,128)S(1)}, f32[256,128]{1,0:T(8,128)S(1)}, u32[]{:S(2)}, u32[]{:S(2)}) %collective-permute-start.23) | collective-permute-done | bytes 131104 | tf_op jit(solution)/shard_map/ppermute | solution.py:334
  80.8 4.3 %collective-permute-done.22 = f32[256,128]{1,0:T(8,128)} collective-permute-done((f32[256,128]{1,0:T(8,128)S(1)}, f32[256,128]{1,0:T(8,128)}, u32[]{:S(2)}, u32[]{:S(2)}) %collective-permute-start.22) | collective-permute-done | bytes 131104 | tf_op jit(solution)/shard_map/ppermute | solution.py:334
  88.0 2.5 %collective-permute-start.24 = (f32[256,128]{1,0:T(8,128)S(1)}, f32[256,128]{1,0:T(8,128)S(1)}, u32[]{:S(2)}, u32[]{:S(2)}) collective-permute-start(f32[256,128]{1,0:T(8,128)S(1)} %fusion.11.refs_1_), channel_id=1, source_target_pairs={{0,2},{1,3},{2,0},{3,1},{4,6},{5,7},{6,4},{7,5},{8,10},{9,11},{10,... | collective-permute-start | bytes 393224 | tf_op jit(solution)/shard_map/ppermute | solution.py:334
  90.5 3.9 %collective-permute-done.26.refs_4_ = f32[256,128]{1,0:T(8,128)S(1)} collective-permute-done((f32[256,128]{1,0:T(8,128)S(1)}, f32[256,128]{1,0:T(8,128)S(1)}, u32[]{:S(2)}, u32[]{:S(2)}) %collective-permute-start.26) | collective-permute-done | bytes 131104 | tf_op jit(solution)/shard_map/ppermute | solution.py:334
  94.4 4.0 %collective-permute-done.25.refs_3_ = f32[256,128]{1,0:T(8,128)S(1)} collective-permute-done((f32[256,128]{1,0:T(8,128)S(1)}, f32[256,128]{1,0:T(8,128)S(1)}, u32[]{:S(2)}, u32[]{:S(2)}) %collective-permute-start.25) | collective-permute-done | bytes 131104 | tf_op jit(solution)/shard_map/ppermute | solution.py:334
  103.3 2.2 %copy-done.1 = bf16[2048,1024]{1,0:T(8,128)(2,1)S(1)} copy-done((bf16[2048,1024]{1,0:T(8,128)(2,1)S(1)}, bf16[2048,1024]{1,0:T(8,128)(2,1)}, u32[]{:S(2)}) %copy-start.1) | copy-done | bytes 4194328
  105.5 2.9 %time_pass.6 = (f32[256,128]{1,0:T(8,128)S(1)}, f32[256,128]{1,0:T(8,128)S(1)}, f32[256,128]{1,0:T(8,128)S(1)}, f32[256,128]{1,0:T(8,128)S(1)}, bf16[2048,128]{1,0:T(8,128)(2,1)S(1)}) custom-call(bf16[2048,1024]{1,0:T(8,128)(2,1)S(1)} %copy-done.1, f32[256,128]{1,0:T(8,128)S(1)} %fusion.11.refs_1_, f32[256,128]{1,0:T(8,128)S(1)} %collective-permute-done.24.refs_2_, ...), custom_call_target="tpu_custom_call" | custom-call | tf_op jit(solution)/shard_map/time_pass/pallas_call | solution.py:204
  112.2 2.3 %collective-permute-done.31 = f32[256,128]{1,0:T(8,128)S(1)} collective-permute-done((f32[256,128]{1,0:T(8,128)S(1)}, f32[256,128]{1,0:T(8,128)S(1)}, u32[]{:S(2)}, u32[]{:S(2)}) %collective-permute-start.31) | collective-permute-done | bytes 131104 | tf_op jit(solution)/shard_map/ppermute | solution.py:334
  114.5 3.4 %collective-permute-done.32 = f32[256,128]{1,0:T(8,128)S(1)} collective-permute-done((f32[256,128]{1,0:T(8,128)S(1)}, f32[256,128]{1,0:T(8,128)S(1)}, u32[]{:S(2)}, u32[]{:S(2)}) %collective-permute-start.32) | collective-permute-done | bytes 131104 | tf_op jit(solution)/shard_map/ppermute | solution.py:334
  121.6 3.3 %collective-permute-done.40.refs_5_ = f32[256,128]{1,0:T(8,128)S(1)} collective-permute-done((f32[256,128]{1,0:T(8,128)S(1)}, f32[256,128]{1,0:T(8,128)S(1)}, u32[]{:S(2)}, u32[]{:S(2)}) %collective-permute-start.40) | collective-permute-done | bytes 131104 | tf_op jit(solution)/shard_map/ppermute | solution.py:334
  126.3 3.0 %time_pass.7 = (f32[256,128]{1,0:T(8,128)S(1)}, f32[256,128]{1,0:T(8,128)S(1)}, f32[256,128]{1,0:T(8,128)S(1)}, f32[256,128]{1,0:T(8,128)S(1)}, f32[264,128]{1,0...) custom-call(bf16[2048,1024]{1,0:T(8,128)(2,1)S(1)} %copy-done.1, ...), custom_call_target="tpu_custom_call" | custom-call | tf_op jit(solution)/shard_map/time_pass/pallas_call | solution.py:204
  130.0 3.4 %collective-permute-start.46 = (f32[264,128]{1,0:T(8,128)S(1)}, f32[264,128]{1,0:T(8,128)S(1)}, u32[]{:S(2)}, u32[]{:S(2)}) collective-permute-start(f32[264,128]{1,0:T(8,128)S(1)} %get-tuple-element.89), channel_id=1, source_target_pairs={{0,2},{1,3},{2,0},{3,1},{4,6},{5,7},{6,4},{7,5},{8,10},{9,11},{10,... | collective-permute-start | bytes 405512 | tf_op jit(solution)/shard_map/ppermute | solution.py:353
  140.5 2.9 %collective-permute-done.42 = f32[256,128]{1,0:T(8,128)S(1)} collective-permute-done((f32[256,128]{1,0:T(8,128)S(1)}, f32[256,128]{1,0:T(8,128)S(1)}, u32[]{:S(2)}, u32[]{:S(2)}) %collective-permute-start.42) | collective-permute-done | bytes 131104 | tf_op jit(solution)/shard_map/ppermute | solution.py:334
  147.1 3.7 %collective-permute-done.50.refs_5_ = f32[256,128]{1,0:T(8,128)S(1)} collective-permute-done((f32[256,128]{1,0:T(8,128)S(1)}, f32[256,128]{1,0:T(8,128)S(1)}, u32[]{:S(2)}, u32[]{:S(2)}) %collective-permute-start.50) | collective-permute-done | bytes 131104 | tf_op jit(solution)/shard_map/ppermute | solution.py:334
  153.7 2.1 %load_mine.3 = (f32[256,128]{1,0:T(8,128)S(1)}, f32[256,128]{1,0:T(8,128)S(1)}, f32[256,128]{1,0:T(8,128)S(1)}, f32[256,128]{1,0:T(8,128)S(1)}, f32[1024,128]{1,0:T(8,128)}) custom-call(bf16[2048,1024]{1,0:T(8,128)(2,1)S(1)} %copy-done.1, bf16[2048,128]{1,0:T(8,128)(2,1)S(1)} %get-tuple-element.72.refs_1_, f32[256,128]{1,0:T(8,128)S(1)} %multiply_subtract_fusion.refs_2_, ...), custom_call_target="tpu_custom_call" | custom-call | tf_op jit(solution)/shard_map/load_mine/pallas_call | solution.py:256
  155.9 2.1 %collective-permute-start.52 = (f32[256,128]{1,0:T(8,128)S(1)}, f32[256,128]{1,0:T(8,128)S(1)}, u32[]{:S(2)}, u32[]{:S(2)}) collective-permute-start(f32[256,128]{1,0:T(8,128)S(1)} %get-tuple-element.96), channel_id=1, source_target_pairs={{0,2},{1,3},{2,0},{3,1},{4,6},{5,7},{6,4},{7,5},{8,10},{9,11},{10,... | collective-permute-start | bytes 393224 | tf_op jit(solution)/shard_map/ppermute | solution.py:334
  158.0 2.8 %collective-permute-start.54 = (f32[256,128]{1,0:T(8,128)S(1)}, f32[256,128]{1,0:T(8,128)S(1)}, u32[]{:S(2)}, u32[]{:S(2)}) collective-permute-start(f32[256,128]{1,0:T(8,128)S(1)} %get-tuple-element.97), channel_id=1, source_target_pairs={{0,6},{1,7},{2,4},{3,5},{4,2},{5,3},{6,0},{7,1},{8,14},{9,15},{10,... | collective-permute-start | bytes 393224 | tf_op jit(solution)/shard_map/ppermute | solution.py:334
  162.1 5.9 %collective-permute-done.54 = f32[256,128]{1,0:T(8,128)S(1)} collective-permute-done((f32[256,128]{1,0:T(8,128)S(1)}, f32[256,128]{1,0:T(8,128)S(1)}, u32[]{:S(2)}, u32[]{:S(2)}) %collective-permute-start.54) | collective-permute-done | bytes 131104 | tf_op jit(solution)/shard_map/ppermute | solution.py:334
  168.0 4.6 %collective-permute-done.53 = f32[256,128]{1,0:T(8,128)S(1)} collective-permute-done((f32[256,128]{1,0:T(8,128)S(1)}, f32[256,128]{1,0:T(8,128)S(1)}, u32[]{:S(2)}, u32[]{:S(2)}) %collective-permute-start.53) | collective-permute-done | bytes 131104 | tf_op jit(solution)/shard_map/ppermute | solution.py:334
  174.7 2.4 %collective-permute-start.55 = (f32[256,128]{1,0:T(8,128)S(1)}, f32[256,128]{1,0:T(8,128)S(1)}, u32[]{:S(2)}, u32[]{:S(2)}) collective-permute-start(f32[256,128]{1,0:T(8,128)S(1)} %fusion.5.refs_0_), channel_id=1, source_target_pairs={{0,2},{1,3},{2,0},{3,1},{4,6},{5,7},{6,4},{7,5},{8,10},{9,11},{10,... | collective-permute-start | bytes 393224 | tf_op jit(solution)/shard_map/ppermute | solution.py:334
  177.1 3.9 %collective-permute-done.57.refs_3_ = f32[256,128]{1,0:T(8,128)S(1)} collective-permute-done((f32[256,128]{1,0:T(8,128)S(1)}, f32[256,128]{1,0:T(8,128)S(1)}, u32[]{:S(2)}, u32[]{:S(2)}) %collective-permute-start.57) | collective-permute-done | bytes 131104 | tf_op jit(solution)/shard_map/ppermute | solution.py:334
  180.9 4.1 %collective-permute-done.56.refs_2_ = f32[256,128]{1,0:T(8,128)S(1)} collective-permute-done((f32[256,128]{1,0:T(8,128)S(1)}, f32[256,128]{1,0:T(8,128)S(1)}, u32[]{:S(2)}, u32[]{:S(2)}) %collective-permute-start.56) | collective-permute-done | bytes 131104 | tf_op jit(solution)/shard_map/ppermute | solution.py:334
  (123 shorter events, 70.8 us)
Async XLA Ops:
  9.1 7.9 %collective-permute-start.3 = (f32[264,128]{1,0:T(8,128)}, f32[264,128]{1,0:T(8,128)S(1)}, u32[]{:S(2)}, u32[]{:S(2)}) collective-permute-start(f32[264,128]{1,0:T(8,128)} %get-tuple-element.55), channel_id=1, source_target_pairs={{0,1},{1,0},{2,3},{3,2},{4,5},{5,4},{6,7},{7,6},{8,9},{9,8},{10,11... | collective-permute-start | bytes 405512 | tf_op jit(solution)/shard_map/ppermute | solution.py:353
  9.7 8.8 %collective-permute-start.4 = (f32[264,128]{1,0:T(8,128)}, f32[264,128]{1,0:T(8,128)S(1)}, u32[]{:S(2)}, u32[]{:S(2)}) collective-permute-start(f32[264,128]{1,0:T(8,128)} %get-tuple-element.56), channel_id=1, source_target_pairs={{1,2},{2,1},{3,4},{4,3},{5,6},{6,5},{9,10},{10,9},{11,12},{12,11},... | collective-permute-start | bytes 405512 | tf_op jit(solution)/shard_map/ppermute | solution.py:353
  10.4 9.9 %collective-permute-start.5 = (f32[264,128]{1,0:T(8,128)}, f32[264,128]{1,0:T(8,128)S(1)}, u32[]{:S(2)}, u32[]{:S(2)}) collective-permute-start(f32[264,128]{1,0:T(8,128)} %get-tuple-element.57), channel_id=1, source_target_pairs={{0,2},{1,3},{2,0},{3,1},{4,6},{5,7},{6,4},{7,5},{8,10},{9,11},{10,... | collective-permute-start | bytes 405512 | tf_op jit(solution)/shard_map/ppermute | solution.py:353
  17.0 9.0 %collective-permute-start.1 = (f32[256,128]{1,0:T(8,128)}, f32[256,128]{1,0:T(8,128)S(1)}, u32[]{:S(2)}, u32[]{:S(2)}) collective-permute-start(f32[256,128]{1,0:T(8,128)} %get-tuple-element.53), channel_id=1, source_target_pairs={{0,16},{8,24},{16,0},{24,8},{1,17},{9,25},{17,1},{25,9},{2,18},{10... | collective-permute-start | bytes 393224 | tf_op jit(solution)/shard_map/ppermute | solution.py:334
  18.5 7.5 %collective-permute-start.2 = (f32[256,128]{1,0:T(8,128)}, f32[256,128]{1,0:T(8,128)S(1)}, u32[]{:S(2)}, u32[]{:S(2)}) collective-permute-start(f32[256,128]{1,0:T(8,128)} %get-tuple-element.54), channel_id=1, source_target_pairs={{0,24},{8,16},{16,8},{24,0},{1,25},{9,17},{17,9},{25,1},{2,26},{10... | collective-permute-start | bytes 393224 | tf_op jit(solution)/shard_map/ppermute | solution.py:334
  27.1 7.3 %collective-permute-start.9 = (f32[256,128]{1,0:T(8,128)S(1)}, f32[256,128]{1,0:T(8,128)S(1)}, u32[]{:S(2)}, u32[]{:S(2)}) collective-permute-start(f32[256,128]{1,0:T(8,128)S(1)} %multiply_subtract_fusion.3.refs_2_), channel_id=1, source_target_pairs={{0,24},{8,16},{16,8},{24,0},{1,25},{9,17},{17,9},{25,1},{2,26},{10... | collective-permute-start | bytes 393224 | tf_op jit(solution)/shard_map/ppermute | solution.py:334
  28.6 7.3 %collective-permute-start.8 = (f32[256,128]{1,0:T(8,128)S(1)}, f32[256,128]{1,0:T(8,128)S(1)}, u32[]{:S(2)}, u32[]{:S(2)}) collective-permute-start(f32[256,128]{1,0:T(8,128)S(1)} %multiply_subtract_fusion.3.refs_2_), channel_id=1, source_target_pairs={{0,16},{8,24},{16,0},{24,8},{1,17},{9,25},{17,1},{25,9},{2,18},{10... | collective-permute-start | bytes 393224 | tf_op jit(solution)/shard_map/ppermute | solution.py:334
  41.9 9.2 %collective-permute-start.15 = (f32[264,128]{1,0:T(8,128)S(1)}, f32[264,128]{1,0:T(8,128)S(1)}, u32[]{:S(2)}, u32[]{:S(2)}) collective-permute-start(f32[264,128]{1,0:T(8,128)S(1)} %get-tuple-element.66), channel_id=1, source_target_pairs={{0,2},{1,3},{2,0},{3,1},{4,6},{5,7},{6,4},{7,5},{8,10},{9,11},{10,... | collective-permute-start | bytes 405512 | tf_op jit(solution)/shard_map/ppermute | solution.py:353
  47.6 8.0 %collective-permute-start.11 = (f32[256,128]{1,0:T(8,128)S(1)}, f32[256,128]{1,0:T(8,128)S(1)}, u32[]{:S(2)}, u32[]{:S(2)}) collective-permute-start(f32[256,128]{1,0:T(8,128)S(1)} %get-tuple-element.62), channel_id=1, source_target_pairs={{0,16},{8,24},{16,0},{24,8},{1,17},{9,25},{17,1},{25,9},{2,18},{10... | collective-permute-start | bytes 393224 | tf_op jit(solution)/shard_map/ppermute | solution.py:334
  48.1 7.4 %collective-permute-start.12 = (f32[256,128]{1,0:T(8,128)S(1)}, f32[256,128]{1,0:T(8,128)S(1)}, u32[]{:S(2)}, u32[]{:S(2)}) collective-permute-start(f32[256,128]{1,0:T(8,128)S(1)} %get-tuple-element.63), channel_id=1, source_target_pairs={{0,24},{8,16},{16,8},{24,0},{1,25},{9,17},{17,9},{25,1},{2,26},{10... | collective-permute-start | bytes 393224 | tf_op jit(solution)/shard_map/ppermute | solution.py:334
  55.6 7.3 %collective-permute-start.19 = (f32[256,128]{1,0:T(8,128)S(1)}, f32[256,128]{1,0:T(8,128)S(1)}, u32[]{:S(2)}, u32[]{:S(2)}) collective-permute-start(f32[256,128]{1,0:T(8,128)S(1)} %multiply_subtract_fusion.2.refs_2_.refs_9_), channel_id=1, source_target_pairs={{0,24},{8,16},{16,8},{24,0},{1,25},{9,17},{17,9},{25,1},{2,26},{10... | collective-permute-start | bytes 393224 | tf_op jit(solution)/shard_map/ppermute | solution.py:334
  70.2 10.6 %collective-permute-start.23 = (f32[256,128]{1,0:T(8,128)S(1)}, f32[256,128]{1,0:T(8,128)S(1)}, u32[]{:S(2)}, u32[]{:S(2)}) collective-permute-start(f32[256,128]{1,0:T(8,128)S(1)} %get-tuple-element.100), channel_id=1, source_target_pairs={{0,6},{1,7},{2,4},{3,5},{4,2},{5,3},{6,0},{7,1},{8,14},{9,15},{10,... | collective-permute-start | bytes 393224 | tf_op jit(solution)/shard_map/ppermute | solution.py:334
  73.3 11.7 %collective-permute-start.22 = (f32[256,128]{1,0:T(8,128)S(1)}, f32[256,128]{1,0:T(8,128)}, u32[]{:S(2)}, u32[]{:S(2)}) collective-permute-start(f32[256,128]{1,0:T(8,128)S(1)} %get-tuple-element.101), channel_id=1, source_target_pairs={{0,4},{1,5},{2,6},{3,7},{4,0},{5,1},{6,2},{7,3},{8,12},{9,13},{10,... | collective-permute-start | bytes 393224 | tf_op jit(solution)/shard_map/ppermute | solution.py:334
  86.0 8.4 %collective-permute-start.26 = (f32[256,128]{1,0:T(8,128)S(1)}, f32[256,128]{1,0:T(8,128)S(1)}, u32[]{:S(2)}, u32[]{:S(2)}) collective-permute-start(f32[256,128]{1,0:T(8,128)S(1)} %fusion.11.refs_1_), channel_id=1, source_target_pairs={{0,6},{1,7},{2,4},{3,5},{4,2},{5,3},{6,0},{7,1},{8,14},{9,15},{10,... | collective-permute-start | bytes 393224 | tf_op jit(solution)/shard_map/ppermute | solution.py:334
  88.0 10.4 %collective-permute-start.25 = (f32[256,128]{1,0:T(8,128)S(1)}, f32[256,128]{1,0:T(8,128)S(1)}, u32[]{:S(2)}, u32[]{:S(2)}) collective-permute-start(f32[256,128]{1,0:T(8,128)S(1)} %fusion.11.refs_1_), channel_id=1, source_target_pairs={{0,4},{1,5},{2,6},{3,7},{4,0},{5,1},{6,2},{7,3},{8,12},{9,13},{10,... | collective-permute-start | bytes 393224 | tf_op jit(solution)/shard_map/ppermute | solution.py:334
  88.0 10.9 %collective-permute-start.27 = (f32[256,128]{1,0:T(8,128)S(1)}, f32[256,128]{1,0:T(8,128)S(1)}, u32[]{:S(2)}, u32[]{:S(2)}) collective-permute-start(f32[256,128]{1,0:T(8,128)S(1)} %fusion.11.refs_1_), channel_id=1, source_target_pairs={{0,1},{1,0},{2,3},{3,2},{4,5},{5,4},{6,7},{7,6},{8,9},{9,8},{10,11... | collective-permute-start | bytes 393224 | tf_op jit(solution)/shard_map/ppermute | solution.py:334
  88.0 11.5 %collective-permute-start.24 = (f32[256,128]{1,0:T(8,128)S(1)}, f32[256,128]{1,0:T(8,128)S(1)}, u32[]{:S(2)}, u32[]{:S(2)}) collective-permute-start(f32[256,128]{1,0:T(8,128)S(1)} %fusion.11.refs_1_), channel_id=1, source_target_pairs={{0,2},{1,3},{2,0},{3,1},{4,6},{5,7},{6,4},{7,5},{8,10},{9,11},{10,... | collective-permute-start | bytes 393224 | tf_op jit(solution)/shard_map/ppermute | solution.py:334
  98.4 11.5 %collective-permute-start.34 = (f32[264,128]{1,0:T(8,128)S(1)}, f32[264,128]{1,0:T(8,128)S(1)}, u32[]{:S(2)}, u32[]{:S(2)}) collective-permute-start(f32[264,128]{1,0:T(8,128)S(1)} %get-tuple-element.78), channel_id=1, source_target_pairs={{0,1},{1,0},{2,3},{3,2},{4,5},{5,4},{6,7},{7,6},{8,9},{9,8},{10,11... | collective-permute-start | bytes 405512 | tf_op jit(solution)/shard_map/ppermute | solution.py:353
  98.9 11.7 %collective-permute-start.35 = (f32[264,128]{1,0:T(8,128)S(1)}, f32[264,128]{1,0:T(8,128)S(1)}, u32[]{:S(2)}, u32[]{:S(2)}) collective-permute-start(f32[264,128]{1,0:T(8,128)S(1)} %get-tuple-element.79), channel_id=1, source_target_pairs={{1,2},{2,1},{3,4},{4,3},{5,6},{6,5},{9,10},{10,9},{11,12},{12,11},... | collective-permute-start | bytes 405512 | tf_op jit(solution)/shard_map/ppermute | solution.py:353
  100.9 11.1 %collective-permute-start.36 = (f32[264,128]{1,0:T(8,128)S(1)}, f32[264,128]{1,0:T(8,128)S(1)}, u32[]{:S(2)}, u32[]{:S(2)}) collective-permute-start(f32[264,128]{1,0:T(8,128)S(1)} %get-tuple-element.80), channel_id=1, source_target_pairs={{0,2},{1,3},{2,0},{3,1},{4,6},{5,7},{6,4},{7,5},{8,10},{9,11},{10,... | collective-permute-start | bytes 405512 | tf_op jit(solution)/shard_map/ppermute | solution.py:353
  102.6 9.4 %collective-permute-start.37 = (f32[264,128]{1,0:T(8,128)S(1)}, f32[264,128]{1,0:T(8,128)S(1)}, u32[]{:S(2)}, u32[]{:S(2)}) collective-permute-start(f32[264,128]{1,0:T(8,128)S(1)} %get-tuple-element.81), channel_id=1, source_target_pairs={{2,4},{3,5},{4,2},{5,3},{10,12},{11,13},{12,10},{13,11},{18,20},{1... | collective-permute-start | bytes 405512 | tf_op jit(solution)/shard_map/ppermute | solution.py:353
  109.9 8.1 %collective-permute-start.32 = (f32[256,128]{1,0:T(8,128)S(1)}, f32[256,128]{1,0:T(8,128)S(1)}, u32[]{:S(2)}, u32[]{:S(2)}) collective-permute-start(f32[256,128]{1,0:T(8,128)S(1)} %get-tuple-element.76), channel_id=1, source_target_pairs={{0,16},{8,24},{16,0},{24,8},{1,17},{9,25},{17,1},{25,9},{2,18},{10... | collective-permute-start | bytes 393224 | tf_op jit(solution)/shard_map/ppermute | solution.py:334
  110.6 7.4 %collective-permute-start.33 = (f32[256,128]{1,0:T(8,128)S(1)}, f32[256,128]{1,0:T(8,128)S(1)}, u32[]{:S(2)}, u32[]{:S(2)}) collective-permute-start(f32[256,128]{1,0:T(8,128)S(1)} %get-tuple-element.77), channel_id=1, source_target_pairs={{0,24},{8,16},{16,8},{24,0},{1,25},{9,17},{17,9},{25,1},{2,26},{10... | collective-permute-start | bytes 393224 | tf_op jit(solution)/shard_map/ppermute | solution.py:334
  130.0 9.2 %collective-permute-start.46 = (f32[264,128]{1,0:T(8,128)S(1)}, f32[264,128]{1,0:T(8,128)S(1)}, u32[]{:S(2)}, u32[]{:S(2)}) collective-permute-start(f32[264,128]{1,0:T(8,128)S(1)} %get-tuple-element.89), channel_id=1, source_target_pairs={{0,2},{1,3},{2,0},{3,1},{4,6},{5,7},{6,4},{7,5},{8,10},{9,11},{10,... | collective-permute-start | bytes 405512 | tf_op jit(solution)/shard_map/ppermute | solution.py:353
  134.8 8.6 %collective-permute-start.42 = (f32[256,128]{1,0:T(8,128)S(1)}, f32[256,128]{1,0:T(8,128)S(1)}, u32[]{:S(2)}, u32[]{:S(2)}) collective-permute-start(f32[256,128]{1,0:T(8,128)S(1)} %get-tuple-element.85), channel_id=1, source_target_pairs={{0,16},{8,24},{16,0},{24,8},{1,17},{9,25},{17,1},{25,9},{2,18},{10... | collective-permute-start | bytes 393224 | tf_op jit(solution)/shard_map/ppermute | solution.py:334
  136.2 7.3 %collective-permute-start.43 = (f32[256,128]{1,0:T(8,128)S(1)}, f32[256,128]{1,0:T(8,128)S(1)}, u32[]{:S(2)}, u32[]{:S(2)}) collective-permute-start(f32[256,128]{1,0:T(8,128)S(1)} %get-tuple-element.86), channel_id=1, source_target_pairs={{0,24},{8,16},{16,8},{24,0},{1,25},{9,17},{17,9},{25,1},{2,26},{10... | collective-permute-start | bytes 393224 | tf_op jit(solution)/shard_map/ppermute | solution.py:334
  158.0 10.0 %collective-permute-start.54 = (f32[256,128]{1,0:T(8,128)S(1)}, f32[256,128]{1,0:T(8,128)S(1)}, u32[]{:S(2)}, u32[]{:S(2)}) collective-permute-start(f32[256,128]{1,0:T(8,128)S(1)} %get-tuple-element.97), channel_id=1, source_target_pairs={{0,6},{1,7},{2,4},{3,5},{4,2},{5,3},{6,0},{7,1},{8,14},{9,15},{10,... | collective-permute-start | bytes 393224 | tf_op jit(solution)/shard_map/ppermute | solution.py:334
  160.7 11.8 %collective-permute-start.53 = (f32[256,128]{1,0:T(8,128)S(1)}, f32[256,128]{1,0:T(8,128)S(1)}, u32[]{:S(2)}, u32[]{:S(2)}) collective-permute-start(f32[256,128]{1,0:T(8,128)S(1)} %get-tuple-element.98), channel_id=1, source_target_pairs={{0,4},{1,5},{2,6},{3,7},{4,0},{5,1},{6,2},{7,3},{8,12},{9,13},{10,... | collective-permute-start | bytes 393224 | tf_op jit(solution)/shard_map/ppermute | solution.py:334
  172.6 8.3 %collective-permute-start.57 = (f32[256,128]{1,0:T(8,128)S(1)}, f32[256,128]{1,0:T(8,128)S(1)}, u32[]{:S(2)}, u32[]{:S(2)}) collective-permute-start(f32[256,128]{1,0:T(8,128)S(1)} %fusion.5.refs_0_), channel_id=1, source_target_pairs={{0,6},{1,7},{2,4},{3,5},{4,2},{5,3},{6,0},{7,1},{8,14},{9,15},{10,... | collective-permute-start | bytes 393224 | tf_op jit(solution)/shard_map/ppermute | solution.py:334
  174.7 10.4 %collective-permute-start.56 = (f32[256,128]{1,0:T(8,128)S(1)}, f32[256,128]{1,0:T(8,128)S(1)}, u32[]{:S(2)}, u32[]{:S(2)}) collective-permute-start(f32[256,128]{1,0:T(8,128)S(1)} %fusion.5.refs_0_), channel_id=1, source_target_pairs={{0,4},{1,5},{2,6},{3,7},{4,0},{5,1},{6,2},{7,3},{8,12},{9,13},{10,... | collective-permute-start | bytes 393224 | tf_op jit(solution)/shard_map/ppermute | solution.py:334
  174.7 10.4 %collective-permute-start.55 = (f32[256,128]{1,0:T(8,128)S(1)}, f32[256,128]{1,0:T(8,128)S(1)}, u32[]{:S(2)}, u32[]{:S(2)}) collective-permute-start(f32[256,128]{1,0:T(8,128)S(1)} %fusion.5.refs_0_), channel_id=1, source_target_pairs={{0,2},{1,3},{2,0},{3,1},{4,6},{5,7},{6,4},{7,5},{8,10},{9,11},{10,... | collective-permute-start | bytes 393224 | tf_op jit(solution)/shard_map/ppermute | solution.py:334
  177.1 8.5 %collective-permute-start.58 = (f32[256,128]{1,0:T(8,128)S(1)}, f32[256,128]{1,0:T(8,128)S(1)}, u32[]{:S(2)}, u32[]{:S(2)}) collective-permute-start(f32[256,128]{1,0:T(8,128)S(1)} %fusion.5.refs_0_), channel_id=1, source_target_pairs={{0,1},{1,0},{2,3},{3,2},{4,5},{5,4},{6,7},{7,6},{8,9},{9,8},{10,11... | collective-permute-start | bytes 393224 | tf_op jit(solution)/shard_map/ppermute | solution.py:334
  (35 other events, 226.3 us)

commit v3 on v0

v3 whole, which is shorter than its diff:
```python
import jax
import jax.numpy as jnp
from jax import lax
from jax.experimental import pallas as pl
from jax.experimental.pallas import tpu as pltpu
from jax.sharding import PartitionSpec as P


LAG = 1440
OUTER = 2
TIME_STEPS = 2

smooth = 4.0
shrink = 0.1
margin = 32.0
hidden = 64.0
F32 = jnp.float32
BF16 = jnp.bfloat16
VMEM = pl.BlockSpec(memory_space=pltpu.VMEM)
ANY = pl.BlockSpec(memory_space=pl.ANY)


def dot_nt(a, b):
    return lax.dot_general(a, b, (((1,), (1,)), ((), ())), preferred_element_type=F32)


def dot_tn(a, b):
    return lax.dot_general(a, b, (((0,), (0,)), ((), ())), preferred_element_type=F32)


def dot_nn(a, b):
    return lax.dot_general(a, b, (((1,), (0,)), ((), ())), preferred_element_type=F32)


def up8(value):
    return -(-value // 8) * 8


class Plan:
    def __init__(self, n_s, n_t, series, minutes, rank):
        self.n_s, self.n_t, self.series, self.minutes, self.rank = n_s, n_t, series, minutes, rank
        self.rows = minutes // n_s
        self.n_z = n_t // 2
        self.block = series // n_t
        self.half = series // 2
        self.bits = self.n_z.bit_length() - 1
        assert 1 << self.bits == self.n_z
        span = 2 * minutes
        self.parts = []
        for s in range(n_s):
            per_core = []
            for core in range(2):
                first = core * minutes + s * self.rows
                wanted = [("near", first - LAG, self.rows + 1), ("far", first + LAG - 1, self.rows + 1),
                          ("prev", first - 1, 1), ("next", first + self.rows, 1)]
                listed = []
                for kind, row, count in wanted:
                    at = 0
                    while at < count:
                        step = (row + at) // span
                        local = (row + at) % span
                        size = min(count - at, span - local)
                        if step == 0 and local < minutes:
                            size = min(size, minutes - local)
                        listed.append((kind, at, step, local, size))
                        at += size
                assert all(abs(p[2]) <= 1 for p in listed)
                per_core.append(listed)
            self.parts.append(per_core)
        self.messages, longest = [], 8
        for s in range(n_s):
            by_step = {}
            for step in (-1, 1):
                offset, placed = 0, []
                for core in range(2):
                    for kind, at, found, local, size in self.parts[s][core]:
                        if found == step:
                            for low, high in ((0, minutes), (minutes, span)):
                                start, end = max(local, low), min(local + size, high)
                                if start < end:
                                    placed.append((core, kind, at + start - local, start, end - start, offset))
                                    offset += up8(end - start)
                by_step[step] = placed
                longest = max(longest, offset)
            self.messages.append(by_step)
        self.length = longest
        self.pairs = [(t, t + 2 * self.facing(t % 2, t // 2)) for t in range(n_t)
                      if 0 <= t + 2 * self.facing(t % 2, t // 2) < n_t]

    def facing(self, core, z):
        return 1 if (core + z) % 2 == 0 else -1


def chip_rows(plan, own, partner, core, local, size):
    half = local // plan.minutes
    ref = own if half == core else partner
    start = local - half * plan.minutes
    return ref[pl.ds(start, size), :]


def each_place(plan, act):
    s = lax.axis_index("series")
    t = lax.axis_index("tm")
    for value in range(plan.n_s):
        for core in range(2):
            for z in range(2):
                @pl.when(jnp.logical_and(s == value, t % 4 == 2 * z + core))
                def _():
                    act(value, core, plan.facing(core, z))


def call(kernel, ins, out_shape, scratch=(), mib=8):
    single = not isinstance(out_shape, list)
    outs = pl.pallas_call(
        kernel,
        in_specs=[VMEM] * len(ins),
        out_specs=VMEM if single else [VMEM] * len(out_shape),
        out_shape=out_shape,
        scratch_shapes=list(scratch),
        compiler_params=pltpu.CompilerParams(vmem_limit_bytes=mib * 2**20),
    )(*ins)
    return outs if single else list(outs)


def array(rows, rank):
    return jax.ShapeDtypeStruct((rows, rank), F32)


def gather(plan, pieces):
    def kernel(*refs):
        s = lax.axis_index("series")
        for k, ref in enumerate(refs[:-1]):
            start = pl.multiple_of(jnp.bitwise_xor(s, k) * plan.rows, plan.rows)
            refs[-1][pl.ds(start, plan.rows), :] = ref[...]

    return call(kernel, pieces, array(plan.minutes, plan.rank))


def pack(plan, x, partner, ahead):
    def kernel(own_ref, partner_ref, ahead_ref, out):
        def act(s, core, facing):
            for _, kind, at, local, size, offset in plan.messages[s][-facing]:
                out[pl.ds(offset, size), :] = chip_rows(plan, own_ref, partner_ref, core, local, size)

        each_place(plan, act)

    return call(kernel, [x, partner, ahead], array(plan.length, plan.rank))


def smoothing(plan, x, partner, got, shared, lag_weights):
    rows, rank = plan.rows, plan.rank
    total = plan.minutes * plan.n_t

    def kernel(x_ref, partner_ref, got_ref, shared_ref, w_ref, out, own_out, near, far, prev, after):
        s = lax.axis_index("series")
        t = lax.axis_index("tm")
        targets = {"near": near, "far": far, "prev": prev, "next": after}

        def act(value, core, facing):
            for kind, at, step, local, size in plan.parts[value][core]:
                if step == 0:
                    targets[kind][pl.ds(at, size), :] = chip_rows(plan, x_ref, partner_ref, core, local, size)
            for step in (-1, 1):
                ref = got_ref if step == facing else shared_ref
                for for_core, kind, at, local, size, offset in plan.messages[value][step]:
                    if for_core == core:
                        targets[kind][pl.ds(at, size), :] = ref[pl.ds(offset, size), :]

        each_place(plan, act)
        x = x_ref[pl.ds(pl.multiple_of(s * rows, rows), rows), :]
        own_out[...] = x
        place = lax.broadcasted_iota(jnp.int32, (rows, rank), 0)
        back_one = jnp.where(place == 0, prev[0:1, :], pltpu.roll(x, 1, 0))
        ahead_one = jnp.where(place == rows - 1, after[0:1, :], pltpu.roll(x, rows - 1, 0))
        w0 = w_ref[0:1, :]
        w1 = w_ref[1:2, :]
        here = t * plan.minutes + s * rows + place
        resid = x - w0 * back_one - w1 * near[pl.ds(0, rows), :]
        after_one = ahead_one - w0 * x - w1 * near[pl.ds(1, rows), :]
        after_far = far[pl.ds(1, rows), :] - w0 * far[pl.ds(0, rows), :] - w1 * x
        after_one = jnp.where(here + 1 < total, after_one, 0.0)
        after_far = jnp.where(here + LAG < total, after_far, 0.0)
        out[...] = smooth * (resid - w0 * after_one - w1 * after_far)

    tall = pltpu.VMEM((up8(rows + 1), rank), F32)
    one = pltpu.VMEM((8, rank), F32)
    return call(kernel, [x, partner, got, shared, lag_weights], [array(rows, rank)] * 2,
                [tall, tall, one, one])


def residual(prod, obs):
    obs = obs.astype(F32)
    return jnp.where(obs < 0.5 * hidden, prod - obs, 0.0).astype(BF16)


def order(plan, q):
    mirrored = sum(((q >> i) & 1) << (plan.bits - 1 - i) for i in range(plan.bits))
    return mirrored, q


def block_start(plan, other, q):
    t = lax.axis_index("tm")
    side = 1 - t % 2 if other else t % 2
    low, high = order(plan, q)
    z = jnp.bitwise_xor(t // 2, jnp.where(side == 0, low, high))
    return pl.multiple_of(side * plan.half + z * plan.block, plan.block)


def store_blocks(plan, places, refs, out):
    for (other, q, count), ref in zip(places, refs):
        for i in range(count):
            out[pl.ds(block_start(plan, other, q + i), plan.block), :] = (
                ref[pl.ds(i * plan.block, plan.block), :].astype(out.dtype))


def time_pass(plan, data, loads, places, x):
    first = len(data) == 2
    n_s, rows, series, minutes, rank = plan.n_s, plan.rows, plan.series, plan.minutes, plan.rank
    chunk = series // 4
    count = series // chunk
    n_f = len(loads)

    def kernel(*refs):
        refs = list(refs)
        d_refs = [refs.pop(0) for _ in data]
        f_refs = [refs.pop(0) for _ in loads]
        x_ref = refs.pop(0)
        g_refs = [refs.pop(0) for _ in range(n_s)]
        f = refs.pop(0) if n_f > 1 else f_refs[0]
        held = refs.pop(0) if first else d_refs[0]
        acc = refs.pop(0)
        if first:
            seen, sem = refs
            copies = []
            for c in range(count):
                span = pl.ds(c * chunk, chunk)
                copies.append([pltpu.make_async_copy(src.at[span, :], dst.at[span, :], sem.at[i, c])
                               for i, (src, dst) in enumerate(zip(d_refs, (held, seen)))])
            for group in copies:
                for copy in group:
                    copy.start()
        if n_f > 1:
            store_blocks(plan, places, f_refs, f)
        xb = x_ref[...].astype(BF16)
        for c in range(count):
            span = pl.ds(c * chunk, chunk)
            if first:
                for copy in copies[c]:
                    copy.wait()
                held[span, :] = jnp.where(seen[span, :] > 0, held[span, :], jnp.full((), hidden, BF16))
            fb = f[span, :].astype(BF16)
            part = dot_tn(fb, residual(dot_nt(fb, xb), held[span, :]))
            if c == 0:
                acc[...] = part
            else:
                acc[...] += part
        s = lax.axis_index("series")
        for k in range(n_s):
            start = pl.multiple_of(jnp.bitwise_xor(s, k) * rows, 128)
            g_refs[k][...] = acc[:, pl.ds(start, rows)].T

    out_shape = [array(rows, rank)] * n_s
    if n_f > 1:
        out_shape.append(jax.ShapeDtypeStruct((series, rank), BF16))
    if first:
        out_shape.append(jax.ShapeDtypeStruct((series, minutes), BF16))
    scratch = [pltpu.VMEM((rank, minutes), F32)]
    if first:
        scratch += [pltpu.VMEM((series, minutes), BF16), pltpu.SemaphoreType.DMA((2, count))]
    outs = list(pl.pallas_call(
        kernel,
        in_specs=[ANY if first else VMEM] * len(data) + [VMEM] * (n_f + 1),
        out_specs=[VMEM] * len(out_shape),
        out_shape=out_shape,
        scratch_shapes=scratch,
        compiler_params=pltpu.CompilerParams(vmem_limit_bytes=(24 if first else 16) * 2**20),
        name="time_pass",
    )(*data, *loads, x))
    return outs[:n_s], outs[n_s:]


def load_pass(plan, data, f, x, groups):
    block = plan.block

    def kernel(d, f_ref, x_ref, *g_refs):
        xb = x_ref[...].astype(BF16)
        for ref, (other, q, count) in zip(g_refs, groups):
            for i in range(count):
                span = pl.ds(block_start(plan, other, q + i), block)
                rb = residual(dot_nt(f_ref[span, :].astype(BF16), xb), d[span, :])
                ref[pl.ds(i * block, block), :] = dot_nn(rb, xb)

    return call(kernel, [data, f, x],
                [array(count * block, plan.rank) for other, q, count in groups], mib=16)


def update_loads(plan, own, parts, step):
    whole = own.shape[0] > plan.block

    def kernel(*refs):
        own_ref, p_refs, out = refs[0], refs[1:-1], refs[-1]
        total = p_refs[0][...]
        for ref in p_refs[1:]:
            total = total + ref[...]
        old = own_ref[pl.ds(block_start(plan, False, 0), plan.block), :] if whole else own_ref[...]
        out[...] = old - step * (total + shrink * old)

    return call(kernel, [own] + parts, array(plan.block, plan.rank))


def assemble(plan, blocks, places):
    def kernel(*refs):
        store_blocks(plan, places, refs[:-1], refs[-1])

    return call(kernel, blocks, array(plan.series, plan.rank))


def body(observed, mask, loadings, factors, lag_weights):
    n_s, n_t = lax.axis_size("series"), lax.axis_size("tm")
    plan = Plan(n_s, n_t, loadings.shape[0], factors.shape[0], loadings.shape[1])
    step_time = 1.0 / (plan.series * n_s / plan.rank + margin)
    step_load = 1.0 / (plan.minutes * n_t)
    n_z, block, bits = plan.n_z, plan.block, plan.bits

    def swap(value, axis, count, k):
        return lax.ppermute(value, axis, [(i, i ^ k) for i in range(count)])

    def swap_z(value, stage):
        bit = [stage, bits - 1 - stage]
        return lax.ppermute(value, "tm", [(i, i ^ (2 << bit[i % 2])) for i in range(n_t)])

    def smooth_all(x, partner, ahead):
        got = lax.ppermute(pack(plan, x, partner, ahead), "tm", plan.pairs)
        shared = swap(got, "tm", n_t, 1)
        return smoothing(plan, x, partner, got, shared, lag_weights)

    loads, places = [loadings], []
    data = [pltpu.with_memory_space_constraint(a, pltpu.HBM) for a in (observed, mask)]
    own_loads = loadings
    x = factors
    known = None
    for outer in range(OUTER):
        for _ in range(TIME_STEPS):
            partner = swap(x, "tm", n_t, 1) if known is None else None
            grads, extra = time_pass(plan, data, loads, places, x)
            if len(data) > 1:
                data = [extra.pop()]
            if len(loads) > 1:
                loads = [extra.pop()]
            smooth_grad, own = known or smooth_all(x, partner, grads[0])
            known = None
            got = [swap(grads[k], "series", n_s, k) for k in range(1, n_s)]
            share = grads[0]
            for value in got:
                share = share + value
            own = own - step_time * (share + smooth_grad)
            x = gather(plan, [own] + [swap(own, "series", n_s, k) for k in range(1, n_s)])
        top = n_z // 2
        other_high, = load_pass(plan, data[0], loads[0], x, [(True, top, top)])
        crossed_high = swap(other_high, "tm", n_t, 1)
        mine_high, = load_pass(plan, data[0], loads[0], x, [(False, top, top)])
        folded = swap_z(mine_high + crossed_high, 0)
        other_low, mine_low = load_pass(plan, data[0], loads[0], x, [(True, 0, top), (False, 0, top)])
        crossed_low = swap(other_low, "tm", n_t, 1)
        if outer + 1 < OUTER:
            known = smooth_all(x, swap(x, "tm", n_t, 1), mine_low)
        parts = [mine_low, crossed_low, folded]
        for stage in range(1, bits):
            size = n_z >> (stage + 1)
            send = sum(p[size * block:2 * size * block] for p in parts)
            parts = [p[:size * block] for p in parts] + [swap_z(send, stage)]
        own_loads = update_loads(plan, own_loads, parts, step_load)
        loads, places = [own_loads], [(False, 0, 1)]
        for stage in reversed(range(bits)):
            size = n_z >> (stage + 1)
            loads.append(swap_z(jnp.concatenate(loads, 0) if len(loads) > 1 else loads[0], stage))
            places.append((False, size, size))
        loads = loads + [swap(value, "tm", n_t, 1) for value in loads]
        places = places + [(True, q, count) for other, q, count in places]
    return (assemble(plan, loads, places), x)


def solution(mesh):
    in_specs = (P("series", "tm"), P("series", "tm"), P("series", None), P("tm", None), P())
    out_specs = (P("series", None), P("tm", None))
    return jax.shard_map(body, mesh=mesh, in_specs=in_specs, out_specs=out_specs, check_vma=False)
```

time: 335 us -> 198 us (0.59)
  waiting for transfers between devices: 170 us -> 113 us
  matrix products: 47.7 us -> 0 us
  blocking collectives: 40.2 us -> 0 us
  Pallas kernels: 0 us -> 22.9 us
  between operations: 14.6 us -> 0.98 us
  other arithmetic: 8.5 us -> 0.36 us
  starting transfers between devices: 51 us -> 57.2 us
    psum x2 -> x0, waiting for transfers between devices: 116 us -> none  [body(): grad_f = lax.psum(partial_load, 'tm')]
    ppermute x24 -> x54, waiting for transfers between devices: 53.9 us -> 113 us  [the longest x8 49.2 us: swap_z(): lax.ppermute(value, 'tm', [(i, i ^ 2 << bit[i % 2]) for i in range(n_t)])]
    dot_general x6 -> x0, matrix products: 47.7 us -> none  [the longest x4 33.8 us: body(): lax.dot_general(rb, fb, (((0,), (0,)), ((), ())), preferred_element_type=...]
    all_gather x4 -> x0, blocking collectives: 40.2 us -> none  [body(): times = lax.all_gather(updated, 'series', axis=0, tiled=True)]
    pallas_call x0 -> x25, Pallas kernels: none -> 22.9 us  [the longest x4 13.5 us: time_pass(): pl.pallas_call(kernel, in_specs=[ANY if first else VMEM] * len(data) + [V...]
    sub x9 -> x4, other arithmetic: 7.09 us -> 0.17 us  [body(): own = own - step_time * (share + smooth_grad)]
    ppermute x24 -> x54, starting transfers between devices: 50.6 us -> 57.2 us  [the longest x42 32 us: swap(): return lax.ppermute(value, axis, [(i, i ^ k) for i in range(count)])]
  transfers between devices with their start and end apart: 30 -> 54, of which waited for: 17 -> 34; matrix products, arithmetic and copies ran while one was open for 0% -> 0% of each run, Pallas kernels for 0% -> 10%
where the time goes in v3:
time: 198 us
  waiting for transfers between devices  113 us (57%)
  starting transfers between devices  57.2 us (29%)
  Pallas kernels  22.9 us (12%)
  local copies, waits for them, and re-layouts  3.31 us (2%)
    ppermute x8, waiting for transfers between devices, swap_z(): lax.ppermute(value, 'tm', [(i, i ^ 2 << bit[i % 2]) for i in range(n_t)])  49.2 us
    ppermute x42, waiting for transfers between devices, swap(): return lax.ppermute(value, axis, [(i, i ^ k) for i in range(count)])  46.5 us
    ppermute x42, starting transfers between devices, swap(): return lax.ppermute(value, axis, [(i, i ^ k) for i in range(count)])  32 us
    ppermute x4, waiting for transfers between devices, smooth_all(): got = lax.ppermute(pack(plan, x, partner, ahead), 'tm', plan.pairs)  17.5 us
    ppermute x4, starting transfers between devices, smooth_all(): got = lax.ppermute(pack(plan, x, partner, ahead), 'tm', plan.pairs)  15 us
    pallas_call x4, Pallas kernels, time_pass(): pl.pallas_call(kernel, in_specs=[ANY if first else VMEM] * len(data) + [V...  13.5 us
    ppermute x8, starting transfers between devices, swap_z(): lax.ppermute(value, 'tm', [(i, i ^ 2 << bit[i % 2]) for i in range(n_t)])  10.3 us
    pallas_call x21, Pallas kernels, call(): pl.pallas_call(kernel, in_specs=[VMEM] * len(ins), out_specs=VMEM if sing...  9.36 us
  transfers between devices with their start and end apart: 54, of which 34 were waited for; matrix products, arithmetic and copies ran while one was open for 0% of the time, Pallas kernels for 10%

profile of v3, /device:TPU:0, one launch (start us, length us, event | category | flops | bytes accessed | tf_op | source)
XLA Modules:
  0.0 198.1 jit_solution(9107728076240964416)
XLA Ops:
  3.5 4.9 %time_pass.4 = (f32[256,128]{1,0:T(8,128)S(1)}, f32[256,128]{1,0:T(8,128)S(1)}, f32[256,128]{1,0:T(8,128)S(1)}, f32[256,128]{1,0:T(8,128)S(1)}, bf16[2048,1024]{1,0:T(8,128)(2,1)S(1)}) custom-call(bf16[2048,1024]{1,0:T(8,128)(2,1)} %refs_0_.2, bf16[2048,1024]{1,0:T(8,128)(2,1)} %refs_1_.2, f32[2048,128]{1,0:T(8,128)S(1)} %copy-done, f32[1024,128]{1,0:T(8,128)S(1)} %copy-done.3), custom_call_target="tpu_custom_call" | custom-call | tf_op jit(solution)/shard_map/time_pass/pallas_call | solution.py:270
  8.5 4.5 %collective-permute-start.1 = (f32[536,128]{1,0:T(8,128)S(1)}, f32[536,128]{1,0:T(8,128)S(1)}, u32[]{:S(2)}, u32[]{:S(2)}) collective-permute-start(f32[536,128]{1,0:T(8,128)S(1)} %shard_map.68), channel_id=1, source_target_pairs={{0,2},{2,0},{3,5},{4,6},{5,3},{6,4},{8,10},{10,8},{11,13},{12,14},... | collective-permute-start | bytes 823304 | tf_op jit(solution)/shard_map/ppermute | solution.py:333
  13.0 4.5 %collective-permute-done.1.got_ref = f32[536,128]{1,0:T(8,128)S(1)} collective-permute-done((f32[536,128]{1,0:T(8,128)S(1)}, f32[536,128]{1,0:T(8,128)S(1)}, u32[]{:S(2)}, u32[]{:S(2)}) %collective-permute-start.1) | collective-permute-done | bytes 274464 | tf_op jit(solution)/shard_map/ppermute | solution.py:333
  21.2 2.5 %collective-permute-done.3 = f32[256,128]{1,0:T(8,128)S(1)} collective-permute-done((f32[256,128]{1,0:T(8,128)S(1)}, f32[256,128]{1,0:T(8,128)S(1)}, u32[]{:S(2)}, u32[]{:S(2)}) %collective-permute-start.3) | collective-permute-done | bytes 131104 | tf_op jit(solution)/shard_map/ppermute | solution.py:326
  23.7 4.1 %collective-permute-done.4 = f32[256,128]{1,0:T(8,128)S(1)} collective-permute-done((f32[256,128]{1,0:T(8,128)S(1)}, f32[256,128]{1,0:T(8,128)S(1)}, u32[]{:S(2)}, u32[]{:S(2)}) %collective-permute-start.4) | collective-permute-done | bytes 131104 | tf_op jit(solution)/shard_map/ppermute | solution.py:326
  31.5 3.7 %collective-permute-done.8.refs_3_ = f32[256,128]{1,0:T(8,128)S(1)} collective-permute-done((f32[256,128]{1,0:T(8,128)S(1)}, f32[256,128]{1,0:T(8,128)S(1)}, u32[]{:S(2)}, u32[]{:S(2)}) %collective-permute-start.8) | collective-permute-done | bytes 131104 | tf_op jit(solution)/shard_map/ppermute | solution.py:326
  36.7 2.8 %time_pass.5 = (f32[256,128]{1,0:T(8,128)S(1)}, f32[256,128]{1,0:T(8,128)S(1)}, f32[256,128]{1,0:T(8,128)S(1)}, f32[256,128]{1,0:T(8,128)S(1)}) custom-call(bf16[2048,1024]{1,0:T(8,128)(2,1)S(1)} %get-tuple-element.32.refs_0_.d, f32[2048,128]{1,0:T(8,128)S(1)} %copy-done, f32[1024,128]{1,0:T(8,128)S(1)} %shard_map.70.refs_2_.own_ref.x_ref), custom_call_target="tpu_custom_call" | custom-call | tf_op jit(solution)/shard_map/time_pass/pallas_call | solution.py:270
  39.7 3.5 %collective-permute-start.10 = (f32[536,128]{1,0:T(8,128)S(1)}, f32[536,128]{1,0:T(8,128)S(1)}, u32[]{:S(2)}, u32[]{:S(2)}) collective-permute-start(f32[536,128]{1,0:T(8,128)S(1)} %shard_map.71), channel_id=1, source_target_pairs={{0,2},{2,0},{3,5},{4,6},{5,3},{6,4},{8,10},{10,8},{11,13},{12,14},... | collective-permute-start | bytes 823304 | tf_op jit(solution)/shard_map/ppermute | solution.py:333
  43.2 4.9 %collective-permute-done.10.got_ref = f32[536,128]{1,0:T(8,128)S(1)} collective-permute-done((f32[536,128]{1,0:T(8,128)S(1)}, f32[536,128]{1,0:T(8,128)S(1)}, u32[]{:S(2)}, u32[]{:S(2)}) %collective-permute-start.10) | collective-permute-done | bytes 274464 | tf_op jit(solution)/shard_map/ppermute | solution.py:333
  51.8 2.6 %collective-permute-done.12 = f32[256,128]{1,0:T(8,128)S(1)} collective-permute-done((f32[256,128]{1,0:T(8,128)S(1)}, f32[256,128]{1,0:T(8,128)S(1)}, u32[]{:S(2)}, u32[]{:S(2)}) %collective-permute-start.12) | collective-permute-done | bytes 131104 | tf_op jit(solution)/shard_map/ppermute | solution.py:326
  54.5 3.5 %collective-permute-done.13 = f32[256,128]{1,0:T(8,128)S(1)} collective-permute-done((f32[256,128]{1,0:T(8,128)S(1)}, f32[256,128]{1,0:T(8,128)S(1)}, u32[]{:S(2)}, u32[]{:S(2)}) %collective-permute-start.13) | collective-permute-done | bytes 131104 | tf_op jit(solution)/shard_map/ppermute | solution.py:326
  61.5 3.7 %collective-permute-done.17.refs_3_ = f32[256,128]{1,0:T(8,128)S(1)} collective-permute-done((f32[256,128]{1,0:T(8,128)S(1)}, f32[256,128]{1,0:T(8,128)S(1)}, u32[]{:S(2)}, u32[]{:S(2)}) %collective-permute-start.17) | collective-permute-done | bytes 131104 | tf_op jit(solution)/shard_map/ppermute | solution.py:326
  72.6 6.8 %collective-permute-done.20 = f32[512,128]{1,0:T(8,128)S(1)} collective-permute-done((f32[512,128]{1,0:T(8,128)S(1)}, f32[512,128]{1,0:T(8,128)S(1)}, u32[]{:S(2)}, u32[]{:S(2)}) %collective-permute-start.20) | collective-permute-done | bytes 262176 | tf_op jit(solution)/shard_map/ppermute | solution.py:330
  81.1 4.6 %collective-permute-done.21.refs_4_ = f32[256,128]{1,0:T(8,128)S(1)} collective-permute-done((f32[256,128]{1,0:T(8,128)S(1)}, f32[256,128]{1,0:T(8,128)S(1)}, u32[]{:S(2)}, u32[]{:S(2)}) %collective-permute-start.21) | collective-permute-done | bytes 131104 | tf_op jit(solution)/shard_map/ppermute | solution.py:330
  87.1 9.2 %collective-permute-done.22.refs_2_ = f32[256,128]{1,0:T(8,128)S(1)} collective-permute-done((f32[256,128]{1,0:T(8,128)S(1)}, f32[256,128]{1,0:T(8,128)S(1)}, u32[]{:S(2)}, u32[]{:S(2)}) %collective-permute-start.22) | collective-permute-done | bytes 131104 | tf_op jit(solution)/shard_map/ppermute | solution.py:330
  96.7 3.9 %collective-permute-start.28 = (f32[536,128]{1,0:T(8,128)S(1)}, f32[536,128]{1,0:T(8,128)S(1)}, u32[]{:S(2)}, u32[]{:S(2)}) collective-permute-start(f32[536,128]{1,0:T(8,128)S(1)} %shard_map.78), channel_id=1, source_target_pairs={{0,2},{2,0},{3,5},{4,6},{5,3},{6,4},{8,10},{10,8},{11,13},{12,14},... | collective-permute-start | bytes 823304 | tf_op jit(solution)/shard_map/ppermute | solution.py:333
  100.6 2.2 %collective-permute-done.23.refs_3_ = f32[512,128]{1,0:T(8,128)S(1)} collective-permute-done((f32[512,128]{1,0:T(8,128)S(1)}, f32[512,128]{1,0:T(8,128)S(1)}, u32[]{:S(2)}, u32[]{:S(2)}) %collective-permute-start.23) | collective-permute-done | bytes 262176 | tf_op jit(solution)/shard_map/ppermute | solution.py:330
  102.8 2.9 %collective-permute-done.28.got_ref = f32[536,128]{1,0:T(8,128)S(1)} collective-permute-done((f32[536,128]{1,0:T(8,128)S(1)}, f32[536,128]{1,0:T(8,128)S(1)}, u32[]{:S(2)}, u32[]{:S(2)}) %collective-permute-start.28) | collective-permute-done | bytes 274464 | tf_op jit(solution)/shard_map/ppermute | solution.py:333
  107.7 2.9 %time_pass.6 = (f32[256,128]{1,0:T(8,128)S(1)}, f32[256,128]{1,0:T(8,128)S(1)}, f32[256,128]{1,0:T(8,128)S(1)}, f32[256,128]{1,0:T(8,128)S(1)}, bf16[2048,128]{1,0:T(8,128)(2,1)S(1)}) custom-call(bf16[2048,1024]{1,0:T(8,128)(2,1)S(1)} %get-tuple-element.32.refs_0_.d, f32[256,128]{1,0:T(8,128)S(1)} %shard_map.77.refs_1_.refs_0_, ...), custom_call_target="tpu_custom_call" | custom-call | tf_op jit(solution)/shard_map/time_pass/pallas_call | solution.py:270
  114.4 2.6 %collective-permute-done.30 = f32[256,128]{1,0:T(8,128)S(1)} collective-permute-done((f32[256,128]{1,0:T(8,128)S(1)}, f32[256,128]{1,0:T(8,128)S(1)}, u32[]{:S(2)}, u32[]{:S(2)}) %collective-permute-start.30) | collective-permute-done | bytes 131104 | tf_op jit(solution)/shard_map/ppermute | solution.py:326
  117.0 2.3 %collective-permute-done.31 = f32[256,128]{1,0:T(8,128)S(1)} collective-permute-done((f32[256,128]{1,0:T(8,128)S(1)}, f32[256,128]{1,0:T(8,128)S(1)}, u32[]{:S(2)}, u32[]{:S(2)}) %collective-permute-start.31) | collective-permute-done | bytes 131104 | tf_op jit(solution)/shard_map/ppermute | solution.py:326
  122.9 3.4 %collective-permute-done.35.refs_3_ = f32[256,128]{1,0:T(8,128)S(1)} collective-permute-done((f32[256,128]{1,0:T(8,128)S(1)}, f32[256,128]{1,0:T(8,128)S(1)}, u32[]{:S(2)}, u32[]{:S(2)}) %collective-permute-start.35) | collective-permute-done | bytes 131104 | tf_op jit(solution)/shard_map/ppermute | solution.py:326
  127.8 2.8 %time_pass.7 = (f32[256,128]{1,0:T(8,128)S(1)}, f32[256,128]{1,0:T(8,128)S(1)}, f32[256,128]{1,0:T(8,128)S(1)}, f32[256,128]{1,0:T(8,128)S(1)}) custom-call(bf16[2048,1024]{1,0:T(8,128)(2,1)S(1)} %get-tuple-element.32.refs_0_.d, bf16[2048,128]{1,0:T(8,128)(2,1)S(1)} %get-tuple-element.47.refs_1_.f_ref, f32[1024,128]{1,0:T(8,128)S(1)} %shard_map.80.refs_2_.own_ref.x_ref), custom_call_target="tpu_custom_call" | custom-call | tf_op jit(solution)/shard_map/time_pass/pallas_call | solution.py:270
  130.7 3.2 %collective-permute-start.37 = (f32[536,128]{1,0:T(8,128)S(1)}, f32[536,128]{1,0:T(8,128)S(1)}, u32[]{:S(2)}, u32[]{:S(2)}) collective-permute-start(f32[536,128]{1,0:T(8,128)S(1)} %shard_map.81), channel_id=1, source_target_pairs={{0,2},{2,0},{3,5},{4,6},{5,3},{6,4},{8,10},{10,8},{11,13},{12,14},... | collective-permute-start | bytes 823304 | tf_op jit(solution)/shard_map/ppermute | solution.py:333
  133.9 5.2 %collective-permute-done.37.got_ref = f32[536,128]{1,0:T(8,128)S(1)} collective-permute-done((f32[536,128]{1,0:T(8,128)S(1)}, f32[536,128]{1,0:T(8,128)S(1)}, u32[]{:S(2)}, u32[]{:S(2)}) %collective-permute-start.37) | collective-permute-done | bytes 274464 | tf_op jit(solution)/shard_map/ppermute | solution.py:333
  142.9 2.6 %collective-permute-done.39 = f32[256,128]{1,0:T(8,128)S(1)} collective-permute-done((f32[256,128]{1,0:T(8,128)S(1)}, f32[256,128]{1,0:T(8,128)S(1)}, u32[]{:S(2)}, u32[]{:S(2)}) %collective-permute-start.39) | collective-permute-done | bytes 131104 | tf_op jit(solution)/shard_map/ppermute | solution.py:326
  145.5 3.5 %collective-permute-done.40 = f32[256,128]{1,0:T(8,128)S(1)} collective-permute-done((f32[256,128]{1,0:T(8,128)S(1)}, f32[256,128]{1,0:T(8,128)S(1)}, u32[]{:S(2)}, u32[]{:S(2)}) %collective-permute-start.40) | collective-permute-done | bytes 131104 | tf_op jit(solution)/shard_map/ppermute | solution.py:326
  152.6 3.7 %collective-permute-done.44.refs_3_ = f32[256,128]{1,0:T(8,128)S(1)} collective-permute-done((f32[256,128]{1,0:T(8,128)S(1)}, f32[256,128]{1,0:T(8,128)S(1)}, u32[]{:S(2)}, u32[]{:S(2)}) %collective-permute-start.44) | collective-permute-done | bytes 131104 | tf_op jit(solution)/shard_map/ppermute | solution.py:326
  164.5 7.3 %collective-permute-done.47 = f32[512,128]{1,0:T(8,128)S(1)} collective-permute-done((f32[512,128]{1,0:T(8,128)S(1)}, f32[512,128]{1,0:T(8,128)S(1)}, u32[]{:S(2)}, u32[]{:S(2)}) %collective-permute-start.47) | collective-permute-done | bytes 262176 | tf_op jit(solution)/shard_map/ppermute | solution.py:330
  173.7 4.5 %collective-permute-done.48.refs_4_ = f32[256,128]{1,0:T(8,128)S(1)} collective-permute-done((f32[256,128]{1,0:T(8,128)S(1)}, f32[256,128]{1,0:T(8,128)S(1)}, u32[]{:S(2)}, u32[]{:S(2)}) %collective-permute-start.48) | collective-permute-done | bytes 131104 | tf_op jit(solution)/shard_map/ppermute | solution.py:330
  179.8 8.8 %collective-permute-done.49.refs_1_ = f32[256,128]{1,0:T(8,128)S(1)} collective-permute-done((f32[256,128]{1,0:T(8,128)S(1)}, f32[256,128]{1,0:T(8,128)S(1)}, u32[]{:S(2)}, u32[]{:S(2)}) %collective-permute-start.49) | collective-permute-done | bytes 131104 | tf_op jit(solution)/shard_map/ppermute | solution.py:330
  189.3 5.8 %collective-permute-done.50.refs_2_ = f32[512,128]{1,0:T(8,128)S(1)} collective-permute-done((f32[512,128]{1,0:T(8,128)S(1)}, f32[512,128]{1,0:T(8,128)S(1)}, u32[]{:S(2)}, u32[]{:S(2)}) %collective-permute-start.50) | collective-permute-done | bytes 262176 | tf_op jit(solution)/shard_map/ppermute | solution.py:330
  (121 shorter events, 63.6 us)
Async XLA Ops:
  0.6 7.8 %collective-permute-start = (f32[1024,128]{1,0:T(8,128)}, f32[1024,128]{1,0:T(8,128)S(1)}, u32[]{:S(2)}, u32[]{:S(2)}) collective-permute-start(f32[1024,128]{1,0:T(8,128)} %x_ref.1), channel_id=1, source_target_pairs={{0,1},{1,0},{2,3},{3,2},{4,5},{5,4},{6,7},{7,6},{8,9},{9,8},{10,11... | collective-permute-start | bytes 1572872 | tf_op jit(solution)/shard_map/ppermute | solution.py:326
  8.5 8.9 %collective-permute-start.1 = (f32[536,128]{1,0:T(8,128)S(1)}, f32[536,128]{1,0:T(8,128)S(1)}, u32[]{:S(2)}, u32[]{:S(2)}) collective-permute-start(f32[536,128]{1,0:T(8,128)S(1)} %shard_map.68), channel_id=1, source_target_pairs={{0,2},{2,0},{3,5},{4,6},{5,3},{6,4},{8,10},{10,8},{11,13},{12,14},... | collective-permute-start | bytes 823304 | tf_op jit(solution)/shard_map/ppermute | solution.py:333
  19.4 8.4 %collective-permute-start.4 = (f32[256,128]{1,0:T(8,128)S(1)}, f32[256,128]{1,0:T(8,128)S(1)}, u32[]{:S(2)}, u32[]{:S(2)}) collective-permute-start(f32[256,128]{1,0:T(8,128)S(1)} %get-tuple-element.36), channel_id=1, source_target_pairs={{0,16},{8,24},{16,0},{24,8},{1,17},{9,25},{17,1},{25,9},{2,18},{10... | collective-permute-start | bytes 393224 | tf_op jit(solution)/shard_map/ppermute | solution.py:326
  21.0 6.9 %collective-permute-start.5 = (f32[256,128]{1,0:T(8,128)S(1)}, f32[256,128]{1,0:T(8,128)S(1)}, u32[]{:S(2)}, u32[]{:S(2)}) collective-permute-start(f32[256,128]{1,0:T(8,128)S(1)} %get-tuple-element.37), channel_id=1, source_target_pairs={{0,24},{8,16},{16,8},{24,0},{1,25},{9,17},{17,9},{25,1},{2,26},{10... | collective-permute-start | bytes 393224 | tf_op jit(solution)/shard_map/ppermute | solution.py:326
  27.9 7.2 %collective-permute-start.8 = (f32[256,128]{1,0:T(8,128)S(1)}, f32[256,128]{1,0:T(8,128)S(1)}, u32[]{:S(2)}, u32[]{:S(2)}) collective-permute-start(f32[256,128]{1,0:T(8,128)S(1)} %multiply_subtract_fusion.3.refs_0_), channel_id=1, source_target_pairs={{0,24},{8,16},{16,8},{24,0},{1,25},{9,17},{17,9},{25,1},{2,26},{10... | collective-permute-start | bytes 393224 | tf_op jit(solution)/shard_map/ppermute | solution.py:326
  29.5 6.9 %collective-permute-start.7 = (f32[256,128]{1,0:T(8,128)S(1)}, f32[256,128]{1,0:T(8,128)S(1)}, u32[]{:S(2)}, u32[]{:S(2)}) collective-permute-start(f32[256,128]{1,0:T(8,128)S(1)} %multiply_subtract_fusion.3.refs_0_), channel_id=1, source_target_pairs={{0,16},{8,24},{16,0},{24,8},{1,17},{9,25},{17,1},{25,9},{2,18},{10... | collective-permute-start | bytes 393224 | tf_op jit(solution)/shard_map/ppermute | solution.py:326
  39.7 8.4 %collective-permute-start.10 = (f32[536,128]{1,0:T(8,128)S(1)}, f32[536,128]{1,0:T(8,128)S(1)}, u32[]{:S(2)}, u32[]{:S(2)}) collective-permute-start(f32[536,128]{1,0:T(8,128)S(1)} %shard_map.71), channel_id=1, source_target_pairs={{0,2},{2,0},{3,5},{4,6},{5,3},{6,4},{8,10},{10,8},{11,13},{12,14},... | collective-permute-start | bytes 823304 | tf_op jit(solution)/shard_map/ppermute | solution.py:333
  49.5 8.4 %collective-permute-start.13 = (f32[256,128]{1,0:T(8,128)S(1)}, f32[256,128]{1,0:T(8,128)S(1)}, u32[]{:S(2)}, u32[]{:S(2)}) collective-permute-start(f32[256,128]{1,0:T(8,128)S(1)} %get-tuple-element.42), channel_id=1, source_target_pairs={{0,16},{8,24},{16,0},{24,8},{1,17},{9,25},{17,1},{25,9},{2,18},{10... | collective-permute-start | bytes 393224 | tf_op jit(solution)/shard_map/ppermute | solution.py:326
  50.0 7.9 %collective-permute-start.14 = (f32[256,128]{1,0:T(8,128)S(1)}, f32[256,128]{1,0:T(8,128)S(1)}, u32[]{:S(2)}, u32[]{:S(2)}) collective-permute-start(f32[256,128]{1,0:T(8,128)S(1)} %get-tuple-element.43), channel_id=1, source_target_pairs={{0,24},{8,16},{16,8},{24,0},{1,25},{9,17},{17,9},{25,1},{2,26},{10... | collective-permute-start | bytes 393224 | tf_op jit(solution)/shard_map/ppermute | solution.py:326
  58.0 7.2 %collective-permute-start.17 = (f32[256,128]{1,0:T(8,128)S(1)}, f32[256,128]{1,0:T(8,128)S(1)}, u32[]{:S(2)}, u32[]{:S(2)}) collective-permute-start(f32[256,128]{1,0:T(8,128)S(1)} %multiply_subtract_fusion.2.refs_0_), channel_id=1, source_target_pairs={{0,24},{8,16},{16,8},{24,0},{1,25},{9,17},{17,9},{25,1},{2,26},{10... | collective-permute-start | bytes 393224 | tf_op jit(solution)/shard_map/ppermute | solution.py:326
  59.5 7.1 %collective-permute-start.16 = (f32[256,128]{1,0:T(8,128)S(1)}, f32[256,128]{1,0:T(8,128)S(1)}, u32[]{:S(2)}, u32[]{:S(2)}) collective-permute-start(f32[256,128]{1,0:T(8,128)S(1)} %multiply_subtract_fusion.2.refs_0_), channel_id=1, source_target_pairs={{0,16},{8,24},{16,0},{24,8},{1,17},{9,25},{17,1},{25,9},{2,18},{10... | collective-permute-start | bytes 393224 | tf_op jit(solution)/shard_map/ppermute | solution.py:326
  60.1 6.4 %collective-permute-start.15 = (f32[256,128]{1,0:T(8,128)S(1)}, f32[256,128]{1,0:T(8,128)S(1)}, u32[]{:S(2)}, u32[]{:S(2)}) collective-permute-start(f32[256,128]{1,0:T(8,128)S(1)} %multiply_subtract_fusion.2.refs_0_), channel_id=1, source_target_pairs={{0,8},{8,0},{16,24},{24,16},{1,9},{9,1},{17,25},{25,17},{2,10},{10... | collective-permute-start | bytes 393224 | tf_op jit(solution)/shard_map/ppermute | solution.py:326
  70.2 9.2 %collective-permute-start.20 = (f32[512,128]{1,0:T(8,128)S(1)}, f32[512,128]{1,0:T(8,128)S(1)}, u32[]{:S(2)}, u32[]{:S(2)}) collective-permute-start(f32[512,128]{1,0:T(8,128)S(1)} %add.74), channel_id=1, source_target_pairs={{0,2},{1,5},{2,0},{3,7},{4,6},{5,1},{6,4},{7,3},{8,10},{9,13},{10,... | collective-permute-start | bytes 786440 | tf_op jit(solution)/shard_map/ppermute | solution.py:330
  71.8 24.6 %collective-permute-start.27 = (f32[1024,128]{1,0:T(8,128)S(1)}, f32[1024,128]{1,0:T(8,128)S(1)}, u32[]{:S(2)}, u32[]{:S(2)}) collective-permute-start(f32[1024,128]{1,0:T(8,128)S(1)} %shard_map.73.x_ref.refs_7_.own_ref), channel_id=1, source_target_pairs={{0,1},{1,0},{2,3},{3,2},{4,5},{5,4},{6,7},{7,6},{8,9},{9,8},{10,11... | collective-permute-start | bytes 1572872 | tf_op jit(solution)/shard_map/ppermute | solution.py:326
  85.8 10.6 %collective-permute-start.22 = (f32[256,128]{1,0:T(8,128)S(1)}, f32[256,128]{1,0:T(8,128)S(1)}, u32[]{:S(2)}, u32[]{:S(2)}) collective-permute-start(f32[256,128]{1,0:T(8,128)S(1)} %shard_map.77.refs_1_.refs_0_), channel_id=1, source_target_pairs={{0,4},{1,3},{2,6},{3,1},{4,0},{5,7},{6,2},{7,5},{8,12},{9,11},{10,... | collective-permute-start | bytes 393224 | tf_op jit(solution)/shard_map/ppermute | solution.py:330
  96.4 6.4 %collective-permute-start.23 = (f32[512,128]{1,0:T(8,128)S(1)}, f32[512,128]{1,0:T(8,128)S(1)}, u32[]{:S(2)}, u32[]{:S(2)}) collective-permute-start(f32[512,128]{1,0:T(8,128)S(1)} %pad_maximum_fusion), channel_id=1, source_target_pairs={{0,2},{1,5},{2,0},{3,7},{4,6},{5,1},{6,4},{7,3},{8,10},{9,13},{10,... | collective-permute-start | bytes 786440 | tf_op jit(solution)/shard_map/ppermute | solution.py:330
  96.7 9.0 %collective-permute-start.28 = (f32[536,128]{1,0:T(8,128)S(1)}, f32[536,128]{1,0:T(8,128)S(1)}, u32[]{:S(2)}, u32[]{:S(2)}) collective-permute-start(f32[536,128]{1,0:T(8,128)S(1)} %shard_map.78), channel_id=1, source_target_pairs={{0,2},{2,0},{3,5},{4,6},{5,3},{6,4},{8,10},{10,8},{11,13},{12,14},... | collective-permute-start | bytes 823304 | tf_op jit(solution)/shard_map/ppermute | solution.py:333
  105.7 8.4 %collective-permute-start.29 = (f32[536,128]{1,0:T(8,128)S(1)}, f32[536,128]{1,0:T(8,128)S(1)}, u32[]{:S(2)}, u32[]{:S(2)}) collective-permute-start(f32[536,128]{1,0:T(8,128)S(1)} %collective-permute-done.28.got_ref), channel_id=1, source_target_pairs={{0,1},{1,0},{2,3},{3,2},{4,5},{5,4},{6,7},{7,6},{8,9},{9,8},{10,11... | collective-permute-start | bytes 823304 | tf_op jit(solution)/shard_map/ppermute | solution.py:326
  110.6 6.4 %collective-permute-start.30 = (f32[256,128]{1,0:T(8,128)S(1)}, f32[256,128]{1,0:T(8,128)S(1)}, u32[]{:S(2)}, u32[]{:S(2)}) collective-permute-start(f32[256,128]{1,0:T(8,128)S(1)} %get-tuple-element.50), channel_id=1, source_target_pairs={{0,8},{8,0},{16,24},{24,16},{1,9},{9,1},{17,25},{25,17},{2,10},{10... | collective-permute-start | bytes 393224 | tf_op jit(solution)/shard_map/ppermute | solution.py:326
  111.3 8.1 %collective-permute-start.31 = (f32[256,128]{1,0:T(8,128)S(1)}, f32[256,128]{1,0:T(8,128)S(1)}, u32[]{:S(2)}, u32[]{:S(2)}) collective-permute-start(f32[256,128]{1,0:T(8,128)S(1)} %get-tuple-element.51), channel_id=1, source_target_pairs={{0,16},{8,24},{16,0},{24,8},{1,17},{9,25},{17,1},{25,9},{2,18},{10... | collective-permute-start | bytes 393224 | tf_op jit(solution)/shard_map/ppermute | solution.py:326
  112.7 6.6 %collective-permute-start.32 = (f32[256,128]{1,0:T(8,128)S(1)}, f32[256,128]{1,0:T(8,128)S(1)}, u32[]{:S(2)}, u32[]{:S(2)}) collective-permute-start(f32[256,128]{1,0:T(8,128)S(1)} %get-tuple-element.52), channel_id=1, source_target_pairs={{0,24},{8,16},{16,8},{24,0},{1,25},{9,17},{17,9},{25,1},{2,26},{10... | collective-permute-start | bytes 393224 | tf_op jit(solution)/shard_map/ppermute | solution.py:326
  119.4 6.9 %collective-permute-start.35 = (f32[256,128]{1,0:T(8,128)S(1)}, f32[256,128]{1,0:T(8,128)S(1)}, u32[]{:S(2)}, u32[]{:S(2)}) collective-permute-start(f32[256,128]{1,0:T(8,128)S(1)} %multiply_subtract_fusion.1.refs_0_), channel_id=1, source_target_pairs={{0,24},{8,16},{16,8},{24,0},{1,25},{9,17},{17,9},{25,1},{2,26},{10... | collective-permute-start | bytes 393224 | tf_op jit(solution)/shard_map/ppermute | solution.py:326
  120.9 6.6 %collective-permute-start.34 = (f32[256,128]{1,0:T(8,128)S(1)}, f32[256,128]{1,0:T(8,128)S(1)}, u32[]{:S(2)}, u32[]{:S(2)}) collective-permute-start(f32[256,128]{1,0:T(8,128)S(1)} %multiply_subtract_fusion.1.refs_0_), channel_id=1, source_target_pairs={{0,16},{8,24},{16,0},{24,8},{1,17},{9,25},{17,1},{25,9},{2,18},{10... | collective-permute-start | bytes 393224 | tf_op jit(solution)/shard_map/ppermute | solution.py:326
  130.7 8.4 %collective-permute-start.37 = (f32[536,128]{1,0:T(8,128)S(1)}, f32[536,128]{1,0:T(8,128)S(1)}, u32[]{:S(2)}, u32[]{:S(2)}) collective-permute-start(f32[536,128]{1,0:T(8,128)S(1)} %shard_map.81), channel_id=1, source_target_pairs={{0,2},{2,0},{3,5},{4,6},{5,3},{6,4},{8,10},{10,8},{11,13},{12,14},... | collective-permute-start | bytes 823304 | tf_op jit(solution)/shard_map/ppermute | solution.py:333
  140.5 8.4 %collective-permute-start.40 = (f32[256,128]{1,0:T(8,128)S(1)}, f32[256,128]{1,0:T(8,128)S(1)}, u32[]{:S(2)}, u32[]{:S(2)}) collective-permute-start(f32[256,128]{1,0:T(8,128)S(1)} %get-tuple-element.57), channel_id=1, source_target_pairs={{0,16},{8,24},{16,0},{24,8},{1,17},{9,25},{17,1},{25,9},{2,18},{10... | collective-permute-start | bytes 393224 | tf_op jit(solution)/shard_map/ppermute | solution.py:326
  141.1 7.8 %collective-permute-start.41 = (f32[256,128]{1,0:T(8,128)S(1)}, f32[256,128]{1,0:T(8,128)S(1)}, u32[]{:S(2)}, u32[]{:S(2)}) collective-permute-start(f32[256,128]{1,0:T(8,128)S(1)} %get-tuple-element.58), channel_id=1, source_target_pairs={{0,24},{8,16},{16,8},{24,0},{1,25},{9,17},{17,9},{25,1},{2,26},{10... | collective-permute-start | bytes 393224 | tf_op jit(solution)/shard_map/ppermute | solution.py:326
  149.0 7.2 %collective-permute-start.44 = (f32[256,128]{1,0:T(8,128)S(1)}, f32[256,128]{1,0:T(8,128)S(1)}, u32[]{:S(2)}, u32[]{:S(2)}) collective-permute-start(f32[256,128]{1,0:T(8,128)S(1)} %multiply_subtract_fusion.refs_0_), channel_id=1, source_target_pairs={{0,24},{8,16},{16,8},{24,0},{1,25},{9,17},{17,9},{25,1},{2,26},{10... | collective-permute-start | bytes 393224 | tf_op jit(solution)/shard_map/ppermute | solution.py:326
  150.5 7.1 %collective-permute-start.43 = (f32[256,128]{1,0:T(8,128)S(1)}, f32[256,128]{1,0:T(8,128)S(1)}, u32[]{:S(2)}, u32[]{:S(2)}) collective-permute-start(f32[256,128]{1,0:T(8,128)S(1)} %multiply_subtract_fusion.refs_0_), channel_id=1, source_target_pairs={{0,16},{8,24},{16,0},{24,8},{1,17},{9,25},{17,1},{25,9},{2,18},{10... | collective-permute-start | bytes 393224 | tf_op jit(solution)/shard_map/ppermute | solution.py:326
  151.2 6.4 %collective-permute-start.42 = (f32[256,128]{1,0:T(8,128)S(1)}, f32[256,128]{1,0:T(8,128)S(1)}, u32[]{:S(2)}, u32[]{:S(2)}) collective-permute-start(f32[256,128]{1,0:T(8,128)S(1)} %multiply_subtract_fusion.refs_0_), channel_id=1, source_target_pairs={{0,8},{8,0},{16,24},{24,16},{1,9},{9,1},{17,25},{25,17},{2,10},{10... | collective-permute-start | bytes 393224 | tf_op jit(solution)/shard_map/ppermute | solution.py:326
  163.0 8.8 %collective-permute-start.47 = (f32[512,128]{1,0:T(8,128)S(1)}, f32[512,128]{1,0:T(8,128)S(1)}, u32[]{:S(2)}, u32[]{:S(2)}) collective-permute-start(f32[512,128]{1,0:T(8,128)S(1)} %add.85), channel_id=1, source_target_pairs={{0,2},{1,5},{2,0},{3,7},{4,6},{5,1},{6,4},{7,3},{8,10},{9,13},{10,... | collective-permute-start | bytes 786440 | tf_op jit(solution)/shard_map/ppermute | solution.py:330
  178.3 10.4 %collective-permute-start.49 = (f32[256,128]{1,0:T(8,128)S(1)}, f32[256,128]{1,0:T(8,128)S(1)}, u32[]{:S(2)}, u32[]{:S(2)}) collective-permute-start(f32[256,128]{1,0:T(8,128)S(1)} %shard_map.87.refs_0_), channel_id=1, source_target_pairs={{0,4},{1,3},{2,6},{3,1},{4,0},{5,7},{6,2},{7,5},{8,12},{9,11},{10,... | collective-permute-start | bytes 393224 | tf_op jit(solution)/shard_map/ppermute | solution.py:330
  188.7 6.4 %collective-permute-start.50 = (f32[512,128]{1,0:T(8,128)S(1)}, f32[512,128]{1,0:T(8,128)S(1)}, u32[]{:S(2)}, u32[]{:S(2)}) collective-permute-start(f32[512,128]{1,0:T(8,128)S(1)} %pad_maximum_fusion.1), channel_id=1, source_target_pairs={{0,2},{1,5},{2,0},{3,7},{4,6},{5,1},{6,4},{7,3},{8,10},{9,13},{10,... | collective-permute-start | bytes 786440 | tf_op jit(solution)/shard_map/ppermute | solution.py:330
  (27 other events, 105.3 us)
